TPU v7x, 32 devices: a whole 2x2x4 slice. The times are simulated.
32 devices in a mesh: gx: 4 (over x, core), gy: 8 (over z, y).
Axes of the slice: x: 2, y: 2, z: 4, core: 2. Of those that a mesh axis runs over, the one named last changes fastest.
Arguments:
- velocity: float32 [2, 11, 32, 1024], P(None, None, 'gx', 'gy'), may hold values from -6 to 6
- thickness: float32 [32, 1024], P('gx', 'gy'), may hold values from 0.5 to 2
- log_friction: float32 [32, 1024], P('gx', 'gy'), may hold values from -1 to 1
- obs_weight: float32 [32, 1024], P('gx', 'gy'), may hold values from 0.5 to 4
- ice_mask: int32 [32, 1024], P('gx', 'gy'), may hold values 0 or 1
- grounded: int32 [32, 1024], P('gx', 'gy'), may hold values 0 or 1
- probes: float32 [8, 32, 1024], P(None, 'gx', 'gy'), may hold values from -6 to 6
Outputs:
- hess_probe: float32 [8, 32, 1024], P(None, 'gx', 'gy')
All inputs are finite; a program needn't handle non-finite values. No bound on the sum of `ice_mask` or of `grounded` on one device may be relied on, other than what follows from the above.
Results may differ from a plain program's by a relative error of at most 0.0003.
Values sent between devices are 32-bit elements; how exact they have to be, the bound alone decides.
A program may use at most 64 MiB of HBM per device.

v0:
```python
import functools

import jax
import jax.numpy as jnp
from jax import lax
from jax.experimental import pallas as pl
from jax.experimental.pallas import tpu as pltpu
from jax.sharding import PartitionSpec as P

MASS_TERM = 0.1
STRAIN_OFFSET = 0.01
ANISO_X = (4.0, 1.0)
ANISO_Y = (1.0, 4.0)
HIGHEST = lax.Precision.HIGHEST
MESH = pl.DeviceIdType.MESH
PAIR = 2


def round_up(value, step):
    return (value + step - 1) // step * step


def kernel(
    sizes,
    vel_ref, thick_ref, logf_ref, obs_ref, ice_ref, ground_ref, probes_ref,
    out_ref,
    xs1, xr1, ys1, yr1,
    xs2, xr2, ys2, yr2,
    xs3, xr3, ys3, yr3,
    ys4, yr4, ub,
    coef, kzs, ratio, inverse, green, weight, bext, bedge, uedge,
    fields, tile_src, landed,
    send_sem, recv_sem, ar_send, ar_recv,
):
    n_gx, n_gy = sizes
    layers = vel_ref.shape[1]
    rows = vel_ref.shape[2]
    lanes = vel_ref.shape[3]
    probes = probes_ref.shape[0]
    half = probes // 2
    comps = 2 * layers
    last = layers - 1
    ix = lax.axis_index("gx")
    iy = lax.axis_index("gy")
    tile = (rows, lanes)
    lane = lax.broadcasted_iota(jnp.int32, tile, 1)
    sub = lax.broadcasted_iota(jnp.int32, tile, 0)
    slot = ((lane + 1) >> 1) & (lanes // 2 - 1)
    even = (lane & 1) == 0
    lane_first = lane == 0
    lane_last = lane == lanes - 1
    sub_first = sub == 0
    sub_last = sub == rows - 1

    sent = []
    barrier = pltpu.get_barrier_semaphore()
    peers = [
        {"gx": lax.rem(ix + step // n_gy, n_gx), "gy": lax.rem(iy + step % n_gy, n_gy)} for step in range(1, n_gx * n_gy)
    ]
    for peer in peers:
        pl.semaphore_signal(barrier, inc=1, device_id=peer, device_id_type=MESH)

    def transfer(phase, way, src, dst):
        axis, idx, count = ("gx", ix, n_gx) if way < 2 else ("gy", iy, n_gy)
        down = way % 2 == 0
        has_dst = idx > 0 if down else idx < count - 1
        has_src = idx < count - 1 if down else idx > 0
        copy = pltpu.make_async_remote_copy(
            src_ref=src, dst_ref=dst,
            send_sem=send_sem.at[phase, way], recv_sem=recv_sem.at[phase, way],
            device_id={axis: idx - 1 if down else idx + 1}, device_id_type=MESH,
        )
        return copy, dst, has_dst, has_src

    def exchange(phase, x_src, x_dst, y_src, y_dst):
        return (
            transfer(phase, 0, x_src[0], x_dst[1]),
            transfer(phase, 1, x_src[1], x_dst[0]),
            transfer(phase, 2, y_src, y_dst[1]),
            transfer(phase, 3, y_src, y_dst[0]),
        )

    def clear(transfers):
        for _, dst, _, has_src in transfers:
            @pl.when(jnp.logical_not(has_src))
            def _(dst=dst):
                dst[...] = jnp.zeros(dst.shape, jnp.float32)

    def start(transfers):
        for copy, _, has_dst, _ in transfers:
            pl.when(has_dst)(copy.start)

    def finish(transfers):
        for copy, _, has_dst, has_src in transfers:
            pl.when(has_src)(copy.wait_recv)
        sent.extend((copy, has_dst) for copy, _, has_dst, _ in transfers)

    ex1 = exchange(0, (xs1.at[0], xs1.at[1]), (xr1.at[0], xr1.at[1]), ys1, (yr1.at[0], yr1.at[1]))
    ex2 = exchange(1, (xs2.at[0], xs2.at[1]), (xr2.at[0], xr2.at[1]), ys2, (yr2.at[0], yr2.at[1]))
    ex3 = exchange(2, (xs3.at[0], xs3.at[1]), (xr3.at[0], xr3.at[1]), ys3, (yr3.at[0], yr3.at[1]))
    pairs_of_rows = rows // PAIR
    ex_rows = [
        (transfer(3 + p, 0, ub.at[p, 1], ub.at[p, rows + 1]), transfer(3 + p, 1, ub.at[p, rows], ub.at[p, 0]))
        for p in range(2)
    ]
    ex_packs = [
        [
            tuple(
                transfer(
                    3 + p + 2 * t, 2 + w, ys4.at[p, pl.ds(t * probes, probes)],
                    yr4.at[p, 1 - w, pl.ds(t * probes, probes)],
                )
                for w in range(2)
            )
            for t in range(pairs_of_rows)
        ]
        for p in range(2)
    ]

    def pack(tiles):
        packed = tiles[0]
        for m in range(1, len(tiles)):
            packed = jnp.where(slot == m, pltpu.roll(tiles[m], 2 * m, 1), packed)
        return packed

    def merge(south, north):
        return jnp.where(even, pltpu.roll(south, 1, 1), pltpu.roll(north, lanes - 1, 1))

    def unpack(merged, m):
        return merged if m == 0 else pltpu.roll(merged, lanes - 2 * m, 1)

    def west(t, row):
        return jnp.where(sub_first, row, pltpu.roll(t, 1, 0))

    def east(t, row):
        return jnp.where(sub_last, row, pltpu.roll(t, rows - 1, 0))

    def south(t, edge):
        return jnp.where(lane_first, edge, pltpu.roll(t, 1, 1))

    def north(t, edge):
        return jnp.where(lane_last, edge, pltpu.roll(t, lanes - 1, 1))

    def ahead(t, d):
        return t if d == 0 else pltpu.roll(t, probes - d, 0)

    mask = ice_ref[...].astype(jnp.float32)
    friction = mask * ground_ref[...].astype(jnp.float32) * jnp.exp(logf_ref[...])
    wm = obs_ref[...] * mask
    fields[0] = friction
    fields[1] = wm
    natural = [vel_ref[c, l] for c in range(2) for l in range(layers)] + [mask, wm]
    for k, t in enumerate(natural):
        xs1[0, k : k + 1, :] = t[0:1, :]
        xs1[1, k : k + 1, :] = t[rows - 1 : rows, :]
    base1 = round_up(len(natural), 8)
    drive = [friction * vel_ref[c, 0] for c in range(2)]
    for i in range(rows):
        probe = probes_ref[:, i, :]
        for c in range(2):
            bext[0, c, i + 1] = probe * drive[c][i : i + 1, :]
    for c in range(2):
        xs1[0, base1 + c * probes : base1 + (c + 1) * probes, :] = bext[0, c, 1]
        xs1[1, base1 + c * probes : base1 + (c + 1) * probes, :] = bext[0, c, rows]
    ys1[0:rows, :] = pack(natural)
    ys1[rows:, :] = pack([bext[0, c, i + 1] for c in range(2) for i in range(rows)])

    for ex in [ex1, ex2, ex3] + ex_rows + ex_packs[0] + ex_packs[1]:
        clear(ex)
    pl.semaphore_wait(barrier, len(peers))
    start(ex1)
    finish(ex1)

    merged1 = merge(yr1[0, 0:rows, :], yr1[1, 0:rows, :])
    edge1 = [unpack(merged1, k) for k in range(len(natural))]
    mergedb = merge(yr1[0, rows:, :], yr1[1, rows:, :])
    for c in range(2):
        bext[0, c, 0] = xr1[0, base1 + c * probes : base1 + (c + 1) * probes, :]
        bext[0, c, rows + 1] = xr1[1, base1 + c * probes : base1 + (c + 1) * probes, :]
        for i in range(rows):
            bedge[0, c, i] = unpack(mergedb, c * rows + i)

    def around(t, k):
        return (
            west(t, xr1[0, k : k + 1, :]), east(t, xr1[1, k : k + 1, :]),
            south(t, edge1[k]), north(t, edge1[k]),
        )

    inverse_step = last / thick_ref[...]
    half_step = 0.5 * inverse_step
    visc = []
    for l in range(layers):
        grads = []
        for c in range(2):
            w, e, s, n = around(vel_ref[c, l], c * layers + l)
            dz = (vel_ref[c, min(l + 1, last)] - vel_ref[c, max(l - 1, 0)]) * half_step
            grads.append((0.5 * (e - w), 0.5 * (n - s), dz))
        (ux, uy, uz), (vx, vy, vz) = grads
        shear = uy + vx
        strain = ux * ux + vy * vy + ux * vy + 0.25 * (shear * shear) + 0.25 * (uz * uz + vz * vz) + STRAIN_OFFSET
        root = jnp.exp(jnp.log(strain) * (-1.0 / 3.0))
        root = root + root * (1.0 - strain * root * root * root) * (1.0 / 3.0)
        mu = jnp.where(mask > 0.5, 0.5 * root, 0.0)
        visc.append(mu)
        xs2[0, l : l + 1, :] = mu[0:1, :]
        xs2[1, l : l + 1, :] = mu[rows - 1 : rows, :]
    ys2[...] = pack(visc)
    start(ex2)
    mask_w, mask_e, mask_s, mask_n = (0.5 * mask * m for m in around(mask, comps))
    step2 = inverse_step * inverse_step
    kz = [0.5 * (visc[l] + visc[l + 1]) * step2 for l in range(last)]
    for l in range(last):
        kzs[l] = kz[l]
    diag = MASS_TERM * mask + (1.0 - mask)
    finish(ex2)
    merged2 = merge(yr2[0], yr2[1])
    for l in range(layers):
        mu = visc[l]
        edge = unpack(merged2, l)
        coef[0, l] = (mu + west(mu, xr2[0, l : l + 1, :])) * mask_w
        coef[1, l] = (mu + east(mu, xr2[1, l : l + 1, :])) * mask_e
        coef[2, l] = (mu + south(mu, edge)) * mask_s
        coef[3, l] = (mu + north(mu, edge)) * mask_n

    for c in range(2):
        ratios, inverses = [], []
        for l in range(layers):
            pivot = ANISO_X[c] * (coef[0, l] + coef[1, l]) + ANISO_Y[c] * (coef[2, l] + coef[3, l]) + diag
            if l == 0:
                pivot = pivot + friction
            if l > 0:
                pivot = pivot + kz[l - 1]
            if l < last:
                pivot = pivot + kz[l]
            if l > 0:
                pivot = pivot - kz[l - 1] * ratios[-1]
            inv = 1.0 / pivot
            inverses.append(inv)
            inverse[c, l] = inv
            if l < last:
                ratios.append(kz[l] * inv)
                ratio[c, l] = ratios[-1]
        up = [inverses[0]]
        for l in range(1, layers):
            up.append(kz[l - 1] * up[-1] * inverses[l])
        low, top = up[last], inverses[last]
        for l in range(last, -1, -1):
            if l < last:
                low = up[l] + ratios[l] * low
                top = ratios[l] * top
            green[0, c, l] = low
            green[1, c, l] = top
    tiles3 = []
    for p in range(2):
        for c in range(2):
            for l in range(layers):
                k = len(tiles3)
                t = green[p, c, l]
                tiles3.append(t)
                xs3[0, k : k + 1, :] = t[0:1, :]
                xs3[1, k : k + 1, :] = t[rows - 1 : rows, :]
    ys3[...] = pack(tiles3)
    start(ex3)
    finish(ex3)
    merged3 = merge(yr3[0], yr3[1])
    for p in range(2):
        for c in range(2):
            for l in range(layers):
                k = (p * 2 + c) * layers + l
                t = green[p, c, l]
                edge = unpack(merged3, k)
                weight[p, c, 0, l] = ANISO_X[c] * coef[0, l] * west(t, xr3[0, k : k + 1, :])
                weight[p, c, 1, l] = ANISO_X[c] * coef[1, l] * east(t, xr3[1, k : k + 1, :])
                weight[p, c, 2, l] = ANISO_Y[c] * coef[2, l] * south(t, edge)
                weight[p, c, 3, l] = ANISO_Y[c] * coef[3, l] * north(t, edge)

    zero = jnp.zeros((probes, lanes), jnp.float32)

    def outer(acc, left, right):
        return tuple(acc[d] + left * ahead(right, d) for d in range(half + 1))

    def place(grams, g, acc):
        for d in range(half + 1):
            total = jnp.broadcast_to(jnp.sum(acc[d], axis=1, keepdims=True), (probes, lanes))
            grams = jnp.where(lane == g * probes + (sub + d) % probes, total, grams)
            if 0 < d < half:
                moved = pltpu.roll(total, d, 0)
                grams = jnp.where(lane == g * probes + (sub + probes - d) % probes, moved, grams)
        return grams

    def solve(p):
        src = 0 if p == 0 else last
        dst = last - src

        def first(t, accs):
            acc_s, acc_1, acc_2 = accs
            packed = None
            for ii in range(PAIR):
                i = t * PAIR + ii
                for c in range(2):
                    b0 = bext[p, c, i + 1]
                    bw = bext[p, c, i]
                    be = bext[p, c, i + 2]
                    edge = bedge[p, c, i]
                    bs = south(b0, edge)
                    bn = north(b0, edge)
                    lateral, y = [], []
                    for l in range(layers):
                        n1 = (
                            weight[p, c, 0, l, pl.ds(i, 1), :] * bw
                            + weight[p, c, 1, l, pl.ds(i, 1), :] * be
                            + weight[p, c, 2, l, pl.ds(i, 1), :] * bs
                            + weight[p, c, 3, l, pl.ds(i, 1), :] * bn
                        )
                        lateral.append(n1)
                        if l > 0:
                            n1 = n1 + kzs[l - 1, pl.ds(i, 1), :] * y[-1]
                        y.append(n1 * inverse[c, l, pl.ds(i, 1), :])
                    x = y[last]
                    for l in range(last, -1, -1):
                        if l < last:
                            x = y[l] + ratio[c, l, pl.ds(i, 1), :] * x
                        ub[p, i + 1, c * layers + l] = x
                        m = (ii * 2 + c) * layers + l
                        moved = x if m == 0 else pltpu.roll(x, 2 * m, 1)
                        packed = moved if packed is None else jnp.where(slot == m, moved, packed)
                        acc_2 = outer(acc_2, lateral[l], x)
                        if l == src:
                            acc_1 = outer(acc_1, b0, x)
                    acc_s = outer(acc_s, green[p, c, src, pl.ds(i, 1), :] * b0, b0)
            ys4[p, pl.ds(t * probes, probes), :] = packed
            return acc_s, acc_1, acc_2

        none = (zero,) * (half + 1)
        accs = (none, none, none)
        order = [0, pairs_of_rows - 1] + list(range(1, pairs_of_rows - 1))
        for n, t in enumerate(order):
            accs = first(t, accs)
            start(ex_packs[p][t])
            if n == 1:
                start(ex_rows[p])
        grams = jnp.zeros((probes, lanes), jnp.float32)
        for g in range(3):
            grams = place(grams, g, accs[g])
        for t in order:
            finish(ex_packs[p][t])
        finish(ex_rows[p])

        def second(t, acc_3):
            at = pl.ds(pl.multiple_of(t * probes, probes), probes)
            merged = merge(yr4[p, 0, at, :], yr4[p, 1, at, :])
            for ii in range(PAIR):
                i = t * PAIR + ii
                for l in range(layers):
                    cw, ce, cs, cn = (coef[q, l, pl.ds(i, 1), :] for q in range(4))
                    for c in range(2):
                        k = c * layers + l
                        w0 = ub[p, i + 1, k]
                        edge = unpack(merged, ii * comps + k)
                        if l == dst:
                            uedge[c, i] = edge
                        n2 = ANISO_X[c] * (cw * ub[p, i, k] + ce * ub[p, i + 2, k]) + ANISO_Y[c] * (
                            cs * south(w0, edge) + cn * north(w0, edge)
                        )
                        acc_3 = outer(acc_3, n2, w0)
            return acc_3

        acc_3 = lax.fori_loop(0, rows // PAIR, second, none)

        grams = place(grams, 3, acc_3)

        width = 4 * probes
        packed = grams
        for q in range(1, probes // PAIR):
            packed = jnp.where(lane < q * width, packed, pltpu.roll(pltpu.roll(grams, probes - PAIR * q, 0), q * width, 1))
        own = pl.ds((ix * n_gy + iy) * PAIR, PAIR)
        landed[p, own, :] = packed[0:PAIR, :]
        total_rows = pl.ds(0, PAIR * len(peers))
        tile_src[p] = packed[0:PAIR, :]
        for peer in peers:
            pltpu.make_async_remote_copy(
                src_ref=tile_src.at[p], dst_ref=landed.at[p, own], send_sem=ar_send.at[p], recv_sem=ar_recv.at[p],
                device_id=peer, device_id_type=MESH,
            ).start()
        everyone = pltpu.make_async_remote_copy(
            src_ref=landed.at[p, total_rows], dst_ref=landed.at[p, total_rows], send_sem=ar_send.at[p],
            recv_sem=ar_recv.at[p], device_id=peers[0], device_id_type=MESH,
        )
        everyone.wait_recv()
        sent.append((everyone, None))
        parts = [landed[p, k * probes : (k + 1) * probes, :] for k in range(landed.shape[1] // probes)]
        while len(parts) > 1:
            parts = [parts[k] + parts[k + 1] if k + 1 < len(parts) else parts[k] for k in range(0, len(parts), 2)]
        packed = parts[0]
        shift = PAIR
        while shift < probes:
            packed = packed + pltpu.roll(packed, shift, 0)
            shift *= 2
        grams = packed
        for q in range(1, probes // PAIR):
            grams = jnp.where(sub < PAIR * q, grams, pltpu.roll(packed, lanes - q * width, 1))

        diff = grams - pltpu.roll(grams, lanes - probes, 1)
        upper = jnp.where(lane < 2 * probes, diff, pltpu.roll(grams, 2 * probes, 1))
        lower = jnp.where(lane < 2 * probes, pltpu.roll(diff, lanes - probes, 1), pltpu.roll(grams, probes, 1))
        size = 2 * probes
        both = [upper, lower]
        scale = [jnp.sum(jnp.where(lane == sub + h * probes, both[h], 0.0), axis=1, keepdims=True) for h in range(2)]
        for k in range(size):
            h, r = k // probes, k % probes
            row = both[h][r : r + 1, :]
            pivot = row[:, k : k + 1]
            inv = jnp.where(pivot > 1e-6 * scale[h][r : r + 1, :], 1.0 / pivot, 0.0)
            row = row * inv
            for q in range(2):
                updated = both[q] - both[q][:, k : k + 1] * row
                both[q] = jnp.where(sub == r, row, updated) if q == h else updated
        pick = (lane == sub + size).astype(jnp.float32)
        return lax.dot_general(
            pick, jnp.concatenate(both, axis=0), (((1,), (1,)), ((), ())),
            precision=HIGHEST, preferred_element_type=jnp.float32,
        )

    def mix(mixing, pairs):
        stacked = jnp.concatenate([jnp.concatenate(pair, axis=0) for pair in pairs], axis=1)
        mixed = lax.dot_general(
            mixing, stacked, (((1,), (0,)), ((), ())), precision=HIGHEST, preferred_element_type=jnp.float32
        )
        return [mixed[:, k * lanes : (k + 1) * lanes] for k in range(len(pairs))]

    mixing = solve(0)
    wm_edge = edge1[comps + 1]
    for c in range(2):
        k = c * layers + last
        inner = green[0, c, last]
        edge = unpack(merged3, k)
        pairs = [(xr3[0, k : k + 1, :] * bext[0, c, 0], ub[0, 0, k])]
        pairs += [(inner[i : i + 1, :] * bext[0, c, i + 1], ub[0, i + 1, k]) for i in range(rows)]
        pairs += [(xr3[1, k : k + 1, :] * bext[0, c, rows + 1], ub[0, rows + 1, k])]
        pairs += [(edge[i : i + 1, :] * bedge[0, c, i], uedge[c, i]) for i in range(rows)]
        mixed = mix(mixing, pairs)
        bext[1, c, 0] = mixed[0] * xr1[0, comps + 1 : comps + 2, :]
        bext[1, c, rows + 1] = mixed[rows + 1] * xr1[1, comps + 1 : comps + 2, :]
        for i in range(rows):
            bext[1, c, i + 1] = mixed[i + 1] * wm[i : i + 1, :]
            bedge[1, c, i] = mixed[rows + 2 + i] * wm_edge[i : i + 1, :]

    mixing = solve(1)
    results = []
    for c in range(2):
        inner = green[1, c, 0]
        results.append(mix(mixing, [
            (inner[i : i + 1, :] * bext[1, c, i + 1], ub[1, i + 1, c * layers]) for i in range(rows)
        ]))
    for i in range(rows):
        out_ref[:, i, :] = drive[0][i : i + 1, :] * results[0][i] + drive[1][i : i + 1, :] * results[1][i]
    for copy, has_dst in sent:
        if has_dst is None:
            copy.wait_send()
        else:
            pl.when(has_dst)(copy.wait_send)


def body(sizes, velocity, thickness, log_friction, obs_weight, ice_mask, grounded, probes):
    layers, rows, lanes = velocity.shape[1:]
    count = probes.shape[0]
    comps = 2 * layers
    n_gx, n_gy = sizes
    rows1 = round_up(comps + 2, 8) + 2 * count
    rows2 = round_up(layers, 8)
    rows3 = round_up(2 * comps, 8)
    packs = rows // PAIR * count

    def vmem(*shape):
        return pltpu.VMEM(shape, jnp.float32)

    def borders(x_rows, y_rows):
        return [vmem(2, x_rows, lanes), vmem(2, x_rows, lanes), vmem(y_rows, lanes), vmem(2, y_rows, lanes)]

    sem = pltpu.SemaphoreType.DMA
    scratch = (
        borders(rows1, rows + count)
        + borders(rows2, rows)
        + borders(rows3, rows)
        + [vmem(2, packs, lanes), vmem(2, 2, packs, lanes), vmem(2, rows + 2, comps, count, lanes)]
        + [
            vmem(4, layers, rows, lanes), vmem(layers - 1, rows, lanes),
            vmem(2, layers - 1, rows, lanes), vmem(2, layers, rows, lanes),
            vmem(2, 2, layers, rows, lanes), vmem(2, 2, 4, layers, rows, lanes),
            vmem(2, 2, rows + 2, count, lanes), vmem(2, 2, rows, count, lanes), vmem(2, rows, count, lanes),
            vmem(2, rows, lanes), vmem(2, PAIR, lanes), vmem(2, PAIR * n_gx * n_gy, lanes),
        ]
        + [sem((3 + 2 * (rows // PAIR), 4)), sem((3 + 2 * (rows // PAIR), 4)), sem((2,)), sem((2,))]
    )
    return pl.pallas_call(
        functools.partial(kernel, sizes),
        out_shape=jax.ShapeDtypeStruct(probes.shape, jnp.float32),
        in_specs=[pl.BlockSpec(memory_space=pltpu.VMEM)] * 7,
        out_specs=pl.BlockSpec(memory_space=pltpu.VMEM),
        scratch_shapes=scratch,
        compiler_params=pltpu.CompilerParams(collective_id=0, has_side_effects=True),
        name="hessian_probe",
    )(velocity, thickness, log_friction, obs_weight, ice_mask, grounded, probes)


def solution(mesh):
    sizes = (mesh.shape["gx"], mesh.shape["gy"])
    in_specs = (
        P(None, None, "gx", "gy"),
        P("gx", "gy"),
        P("gx", "gy"),
        P("gx", "gy"),
        P("gx", "gy"),
        P("gx", "gy"),
        P(None, "gx", "gy"),
    )
    out_specs = P(None, "gx", "gy")
    return jax.shard_map(
        functools.partial(body, sizes), mesh=mesh, in_specs=in_specs, out_specs=out_specs, check_vma=False
    )
```

profile of v0, /device:TPU:0, one launch (start us, length us, event | category | flops | bytes accessed | tf_op | source)
XLA Modules:
  0.0 43.6 jit_solution(6506068216493430975)
XLA Ops:
  0.0 42.2 %hessian_probe.1 = f32[8,8,128]{2,1,0:T(8,128)} custom-call(f32[2,11,8,128]{3,2,1,0:T(8,128)} %vel_ref.1, f32[8,128]{1,0:T(8,128)} %thick_ref.1, f32[8,128]{1,0:T(8,128)} %logf_ref.1, f32[8,128]{1,0:T(8,128)} %obs_ref.1, s32[8,128]{1,0:T(8,128)} %ice_ref.1, s32[8,128]{1,0:T(8,128)} %ground_ref.1, f32[8,8,128]{2,1,0:T(8,128)} %probes_ref.1), custom_call_target="tpu_custom_call" | custom-call | tf_op jit(solution)/shard_map/hessian_probe/pallas_call | solution.py:495
  42.2 1.4 %copy.9 = f32[8,8,128]{2,1,0:T(8,128)} copy(f32[8,8,128]{2,1,0:T(8,128)} %hessian_probe.1) | data formatting | bytes 65536
where the time goes:
time: 43.8 us; the launch traced here: 43.6 us
  Pallas kernels  42.2 us (96%)
  local copies, waits for them, and re-layouts  1.38 us (3%)
    pallas_call x1, Pallas kernels, body(): pl.pallas_call(functools.partial(kernel, sizes), out_shape=jax.ShapeDtype...  42.2 us
    unnamed x1, local copies, waits for them, and re-layouts  1.38 us

commit v1 on v0

v1 whole, which is shorter than its diff:
```python
import functools

import jax
import jax.numpy as jnp
from jax import lax
from jax.experimental import pallas as pl
from jax.experimental.pallas import tpu as pltpu
from jax.sharding import PartitionSpec as P

MASS_TERM = 0.1
STRAIN_OFFSET = 0.01
ANISO_X = (4.0, 1.0)
ANISO_Y = (1.0, 4.0)
HIGHEST = lax.Precision.HIGHEST
MESH = pl.DeviceIdType.MESH
PAIR = 2
REACH = 5
SLOT = 2 * REACH
WEST, EAST, SOUTH, NORTH = range(4)
DIRS = range(4)
FORMS = 4


class Field:
    def __init__(self, tiles):
        self.tiles = tiles

    def _with(self, other, op):
        if isinstance(other, Field):
            return Field([None if a is None or b is None else op(a, b) for a, b in zip(self.tiles, other.tiles)])
        return Field([None if a is None else op(a, other) for a in self.tiles])

    def __add__(self, other):
        return self._with(other, lambda a, b: a + b)

    def __sub__(self, other):
        return self._with(other, lambda a, b: a - b)

    def __mul__(self, other):
        return self._with(other, lambda a, b: a * b)

    __radd__ = __add__
    __rmul__ = __mul__

    def map(self, op):
        return Field([None if a is None else op(a) for a in self.tiles])


def kernel(
    sizes,
    vel_ref, thick_ref, logf_ref, obs_ref, ice_ref, ground_ref, probes_ref,
    out_ref,
    row, hrow, tn, ts, edge_src, edge_dst,
    coef, kzs, ratio, inverse, green, wsc, hsc, hshift, quad, drv, wmx, probe_strip,
    bx, left, right, basis, results, tile_src, landed,
    send_sem, recv_sem, ar_send, ar_recv,
):
    n_gx, n_gy = sizes
    layers = vel_ref.shape[1]
    rows = vel_ref.shape[2]
    lanes = vel_ref.shape[3]
    probes = probes_ref.shape[0]
    last = layers - 1
    half = rows // 2
    per_tile = layers + 1
    n_fields = 2 * per_tile + probes + 2
    ix = lax.axis_index("gx")
    iy = lax.axis_index("gy")
    tile = (rows, lanes)
    lane = lax.broadcasted_iota(jnp.int32, tile, 1)
    sub = lax.broadcasted_iota(jnp.int32, tile, 0)
    lane_first = lane == 0
    lane_last = lane == lanes - 1
    sub_first = sub == 0
    sub_last = sub == rows - 1
    slot_id = lane // SLOT
    high = lane - slot_id * SLOT < REACH

    barrier = pltpu.get_barrier_semaphore()
    peers = [
        {"gx": lax.rem(ix + step // n_gy, n_gx), "gy": lax.rem(iy + step % n_gy, n_gy)} for step in range(1, n_gx * n_gy)
    ]
    for peer in peers:
        pl.semaphore_signal(barrier, inc=1, device_id=peer, device_id_type=MESH)

    def lane_roll(t, shift):
        shift = shift % lanes
        return t if shift == 0 else pltpu.roll(t, shift, 1)

    def sub_roll(t, shift):
        return pltpu.roll(t, shift % rows, 0)

    def inside(dx, dy):
        tests = []
        if dx:
            tests.append(ix > 0 if dx < 0 else ix < n_gx - 1)
        if dy:
            tests.append(iy > 0 if dy < 0 else iy < n_gy - 1)
        return functools.reduce(jnp.logical_and, tests)

    def transfer(k, dx, dy, src, dst):
        target = {}
        if dx:
            target["gx"] = ix + dx
        if dy:
            target["gy"] = iy + dy
        copy = pltpu.make_async_remote_copy(
            src_ref=src, dst_ref=dst, send_sem=send_sem.at[k], recv_sem=recv_sem.at[k],
            device_id=target, device_id_type=MESH,
        )
        return copy, dst, inside(dx, dy), inside(-dx, -dy)

    low, top = pl.ds(0, half), pl.ds(half, half)
    corner_low, corner_top = pl.ds(rows, half), pl.ds(rows + half, half)
    own_pack = pl.ds(n_fields, 3)
    whole = pl.ds(0, rows)
    everything = pl.ds(0, n_fields + 3)
    packs = pl.ds(0, 3)
    exchange = [
        transfer(0, -1, 0, row.at[everything, low], hrow.at[everything, low]),
        transfer(1, 1, 0, row.at[everything, top], hrow.at[everything, top]),
        transfer(2, 0, -1, row.at[own_pack, whole], tn.at[packs, whole]),
        transfer(3, 0, 1, row.at[own_pack, whole], ts.at[packs, whole]),
        transfer(4, -1, -1, row.at[own_pack, low], tn.at[packs, corner_low]),
        transfer(5, 1, -1, row.at[own_pack, top], tn.at[packs, corner_top]),
        transfer(6, -1, 1, row.at[own_pack, low], ts.at[packs, corner_low]),
        transfer(7, 1, 1, row.at[own_pack, top], ts.at[packs, corner_top]),
    ]
    edge_copy = transfer(8, -1, 0, edge_src, edge_dst)

    mask_own = ice_ref[...].astype(jnp.float32)
    friction_own = mask_own * ground_ref[...].astype(jnp.float32) * jnp.exp(logf_ref[...])
    wm_own = obs_ref[...] * mask_own
    own = [vel_ref[0, l] for l in range(layers)] + [thick_ref[...]]
    own += [vel_ref[1, l] for l in range(layers)] + [mask_own]
    own += [probes_ref[p] for p in range(probes)] + [friction_own, wm_own]
    for f, t in enumerate(own):
        row[f] = t
    for k in range(3):
        packed = None
        for s, t in enumerate(own[k * per_tile : (k + 1) * per_tile]):
            moved = lane_roll(t, s * SLOT + REACH)
            packed = moved if packed is None else jnp.where(slot_id == s, moved, packed)
        row[n_fields + k] = packed

    for _, dst, _, has_src in exchange + [edge_copy]:
        @pl.when(jnp.logical_not(has_src))
        def _(dst=dst):
            dst[...] = jnp.zeros(dst.shape, jnp.float32)
    pl.semaphore_wait(barrier, len(peers))
    for copy, _, has_dst, _ in exchange:
        pl.when(has_dst)(copy.start)
    for copy, _, _, has_src in exchange:
        pl.when(has_src)(copy.wait_recv)

    def shifted(f, axis, forward):
        if axis == 0:
            at, move, pairs = (sub_first, -1, ((0, 1), (1, 0), (2, 3), (3, 2))) if forward else (sub_last, 1, ((0, 1), (1, 0), (2, 3), (3, 2)))
            roll = sub_roll
        else:
            at, move, pairs = (lane_first, -1, ((0, 2), (1, 3), (2, 0), (3, 1))) if forward else (lane_last, 1, ((0, 2), (1, 3), (2, 0), (3, 1)))
            roll = lane_roll
        tiles = [None] * 4
        for a, b in pairs:
            if f.tiles[a] is not None and f.tiles[b] is not None:
                tiles[a] = roll(jnp.where(at, f.tiles[b], f.tiles[a]), move)
        return Field(tiles)

    def neighbour(f, d):
        return shifted(f, 0 if d in (WEST, EAST) else 1, d in (EAST, NORTH))

    both_packs = [
        [jnp.where(high, ts[k, pl.ds(h * rows, rows), :], tn[k, pl.ds(h * rows, rows), :]) for h in range(2)]
        for k in range(3)
    ]

    def strip(packs_of, s):
        return [lane_roll(t, -(s * SLOT + REACH)) for t in packs_of]

    def assemble(f):
        return Field([own[f], hrow[f]] + strip(both_packs[f // per_tile], f % per_tile))

    thick = assemble(layers).map(lambda t: jnp.where(t > 0.0, t, 1.0))
    inverse_step = thick.map(lambda t: last / t)
    mask = assemble(per_tile + layers)
    friction = assemble(2 * per_tile + probes)
    wm = assemble(2 * per_tile + probes + 1)

    def viscosity(ux, uy, uz, vx, vy, vz):
        shear = uy + vx
        strain = ux * ux + vy * vy + ux * vy + 0.25 * (shear * shear) + 0.25 * (uz * uz + vz * vz) + STRAIN_OFFSET
        root = jnp.exp(jnp.log(strain) * (-1.0 / 3.0))
        root = root + root * (1.0 - strain * root * root * root) * (1.0 / 3.0)
        return 0.5 * root

    strips = []
    for north_side in (True, False):
        def side(k):
            tiles = []
            for h in range(2):
                mine = row[n_fields + k] if h == 0 else hrow[n_fields + k]
                theirs = (tn if north_side else ts)[k, pl.ds(h * rows, rows), :]
                tiles.append(jnp.where(high, mine, theirs) if north_side else jnp.where(high, theirs, mine))
            return tiles
        u_side, v_side = side(0), side(1)
        steps = []
        for t in u_side:
            t = jnp.where(t > 0.0, t, 1.0)
            have = 1
            while have < per_tile:
                t = jnp.where(slot_id >= per_tile - have, t, lane_roll(t, -SLOT * have))
                have *= 2
            steps.append((0.5 * last) / t)
        mu = []
        grads = []
        for pair in (u_side, v_side):
            e = [sub_roll(jnp.where(sub_first, pair[1 - h], pair[h]), -1) for h in range(2)]
            w = [sub_roll(jnp.where(sub_last, pair[1 - h], pair[h]), 1) for h in range(2)]
            for h in range(2):
                t = pair[h]
                n, s = lane_roll(t, -1), lane_roll(t, 1)
                above = jnp.where(slot_id == last, t, lane_roll(t, -SLOT))
                below = jnp.where(slot_id == 0, t, lane_roll(t, SLOT))
                grads.append((0.5 * (e[h] - w[h]), 0.5 * (n - s), (above - below) * steps[h]))
        for h in range(2):
            mu.append(viscosity(*grads[h], *grads[2 + h]))
        strips.append(mu)
    mu_packs = [jnp.where(high, strips[1][h], strips[0][h]) for h in range(2)]

    half_step = Field((0.5 * inverse_step).tiles[:2] + [None, None])
    velocity = []
    for c in range(2):
        for l in range(layers):
            velocity.append(assemble(c * per_tile + l))
    visc = []
    for l in range(layers):
        grads = []
        for c in range(2):
            f = velocity[c * layers + l]
            main = Field(f.tiles[:2] + [None, None])
            gx = 0.5 * (neighbour(main, EAST) - neighbour(main, WEST))
            gy = 0.5 * (neighbour(f, NORTH) - neighbour(f, SOUTH))
            gz = (velocity[c * layers + min(l + 1, last)] - velocity[c * layers + max(l - 1, 0)]) * half_step
            grads.append((gx, gy, gz))
        (ux, uy, uz), (vx, vy, vz) = grads
        tiles = [
            viscosity(ux.tiles[h], uy.tiles[h], uz.tiles[h], vx.tiles[h], vy.tiles[h], vz.tiles[h]) for h in range(2)
        ]
        visc.append(Field(tiles + strip(mu_packs, l)))

    def store(ref, index, f):
        for k, t in enumerate(f.tiles):
            if t is not None:
                ref[index + (k,)] = t

    def load(ref, index, count=4):
        return Field([ref[index + (k,)] if k < count else None for k in range(4)])

    for c in range(2):
        store(drv, (c,), friction * velocity[c * layers])
    store(wmx, (), wm)
    for p in range(probes):
        for h, t in enumerate(strip(both_packs[2], p)):
            probe_strip[p, pl.ds(h * rows, rows), :] = t

    mask_e = 0.5 * (mask * neighbour(mask, EAST))
    mask_n = 0.5 * (mask * neighbour(mask, NORTH))
    step2 = 0.5 * (inverse_step * inverse_step * mask)
    diag = MASS_TERM * mask + mask.map(lambda t: 1.0 - t)
    for l in range(layers):
        mu = visc[l]
        k_e = (mu + neighbour(mu, EAST)) * mask_e
        k_n = (mu + neighbour(mu, NORTH)) * mask_n
        for d, f in ((WEST, neighbour(k_e, WEST)), (EAST, k_e), (SOUTH, neighbour(k_n, SOUTH)), (NORTH, k_n)):
            store(coef, (d, l), f)
        if l < last:
            store(kzs, (l,), (mu + visc[l + 1]) * step2)

    for c in range(2):
        ratios, inverses = [], []
        for l in range(layers):
            k = [load(coef, (d, l)) for d in DIRS]
            pivot = ANISO_X[c] * (k[WEST] + k[EAST]) + ANISO_Y[c] * (k[SOUTH] + k[NORTH]) + diag
            if l == 0:
                pivot = pivot + friction
            if l > 0:
                below = load(kzs, (l - 1,))
                pivot = pivot + below
            if l < last:
                pivot = pivot + load(kzs, (l,))
            if l > 0:
                pivot = pivot - below * ratios[-1]
            inv = pivot.map(lambda t: 1.0 / t)
            inverses.append(inv)
            store(inverse, (c, l), inv)
            if l < last:
                ratios.append(load(kzs, (l,)) * inv)
                store(ratio, (c, l), ratios[-1])
        up = [inverses[0]]
        for l in range(1, layers):
            up.append(load(kzs, (l - 1,)) * up[-1] * inverses[l])
        from_bottom, from_top = up[last], inverses[last]
        for l in range(last, -1, -1):
            if l < last:
                from_bottom = up[l] + ratios[l] * from_bottom
                from_top = ratios[l] * from_top
            store(green, (0, c, l), from_bottom)
            store(green, (1, c, l), from_top)

    def prepare(p):
        src = 0 if p == 0 else last
        for c in range(2):
            scale = (ANISO_X[c], ANISO_X[c], ANISO_Y[c], ANISO_Y[c])
            for d in DIRS:
                y = []
                for l in range(layers):
                    w = scale[d] * (load(coef, (d, l)) * neighbour(load(green, (p, c, l)), d))
                    wsc[c, d, l] = w.tiles[0]
                    if p == 1:
                        w = Field(w.tiles[:3] + [None])
                    if l > 0:
                        w = w + load(kzs, (l - 1,)) * y[-1]
                    y.append(w * load(inverse, (c, l)))
                x = y[last]
                for l in range(last, -1, -1):
                    if l < last:
                        x = Field((y[l] + load(ratio, (c, l)) * x).tiles[:3] + [None])
                    store(hsc, (p, c, d, l), x)
                    hshift[c, 0, d, l] = sub_roll(jnp.where(sub_first, x.tiles[1], x.tiles[0]), -1)
                    hshift[c, 1, d, l] = lane_roll(jnp.where(lane_first, x.tiles[2], x.tiles[0]), -1)
            quad[p, c, 0] = green[p, c, src, 0]
            for d in DIRS:
                quad[p, c, 1 + d] = hsc[p, c, d, src, 0]
            at = 1 + len(DIRS)
            for d in DIRS:
                for e in range(d, 4):
                    total = None
                    for l in range(layers):
                        term = wsc[c, d, l] * hsc[p, c, e, l, 0]
                        total = term if total is None else total + term
                    quad[p, c, at] = total
                    at += 1
            for d in DIRS:
                total = [None] * 6
                for l in range(layers):
                    h = hsc[p, c, d, l, 0]
                    t_e = (ANISO_X[c] * coef[EAST, l, 0]) * h
                    t_n = (ANISO_Y[c] * coef[NORTH, l, 0]) * h
                    he = [hshift[c, 0, e, l] for e in DIRS]
                    hn = [hshift[c, 1, e, l] for e in DIRS]
                    terms = [
                        t_e * he[WEST] + t_n * hn[SOUTH], t_e * he[EAST], t_e * he[SOUTH],
                        t_e * he[NORTH] + t_n * hn[EAST], t_n * hn[WEST], t_n * hn[NORTH],
                    ]
                    total = [b if a is None else a + b for a, b in zip(total, terms)]
                for k in range(6):
                    quad[p, c, at] = total[k]
                    at += 1

    def where_row(r):
        return (0, r) if 0 <= r < rows else (1, r % rows)

    def main_strip(ref, index, r):
        h, at = where_row(r)
        return ref[index + (h, pl.ds(at, 1), slice(None))], ref[index + (2 + h, pl.ds(at, 1), slice(None))]

    def north_of(m, s):
        return lane_roll(jnp.where(lane_first, s, m), -1)

    def south_of(m, s):
        return lane_roll(jnp.where(lane_last, s, m), 1)

    def b_of(p, c, r, s=0):
        return bx[p, c, r + 2, s]

    def grams_of(p):
        for c in range(2):
            for i in range(rows):
                k = pl.ds((c * rows + i) * lanes, lanes)
                q = quad.at[p, c]

                def row_of(index):
                    return q[index, pl.ds(i, 1), :]

                b0 = b_of(p, c, i)
                n_w, n_0, n_e = (north_of(b_of(p, c, i + d), b_of(p, c, i + d, 1)) for d in (-1, 0, 1))
                s_0, s_e = (south_of(b_of(p, c, i + d), b_of(p, c, i + d, 1)) for d in (0, 1))
                n_2 = lane_roll(jnp.where(lane < 2, b_of(p, c, i, 1), b0), -2)
                around = [b_of(p, c, i - 1), b_of(p, c, i + 1), s_0, n_0]
                far = [b0, b_of(p, c, i + 2), s_e, n_e, n_w, n_2]
                left[0, :, k] = b0
                right[0, 0:probes, k] = row_of(0) * b0
                first = [row_of(1 + d) * around[d] for d in DIRS]
                right[0, probes:, k] = (first[0] + first[1]) + (first[2] + first[3])
                at = 1 + len(DIRS)
                cross = {}
                for d in DIRS:
                    for e in range(d, 4):
                        cross[d, e] = cross[e, d] = row_of(at)
                        at += 1
                for d in DIRS:
                    left[1 + d, :, k] = around[d]
                    terms = [cross[d, e] * around[e] for e in DIRS]
                    right[1 + d, 0:probes, k] = (terms[0] + terms[1]) + (terms[2] + terms[3])
                    terms = [row_of(at + j) * far[j] for j in range(6)]
                    at += 6
                    right[1 + d, probes:, k] = (terms[0] + terms[1]) + (terms[2] + terms[3]) + (terms[4] + terms[5])
        dots = [
            lax.dot_general(
                left[k], right[k], (((1,), (1,)), ((), ())), precision=HIGHEST, preferred_element_type=jnp.float32
            )
            for k in range(5)
        ]
        outer = (dots[1] + dots[2]) + (dots[3] + dots[4])
        pad = jnp.zeros((probes, lanes - FORMS * probes), jnp.float32)
        return jnp.concatenate([dots[0], outer, pad], axis=1)

    def start_sum(p, grams):
        base = (FORMS - 1) * probes
        mirrored = grams
        for r in range(probes):
            column = jnp.sum(
                jnp.where(lane == base + sub, jnp.broadcast_to(grams[r : r + 1, :], tile), 0.0), axis=1, keepdims=True
            )
            mirrored = jnp.where(lane == base + r, grams + column, mirrored)
        grams = mirrored
        width = FORMS * probes
        packed = grams
        for q in range(1, probes // PAIR):
            packed = jnp.where(lane < q * width, packed, lane_roll(sub_roll(grams, -PAIR * q), q * width))
        mine = pl.ds((ix * n_gy + iy) * PAIR, PAIR)
        landed[p, mine, :] = packed[0:PAIR, :]
        tile_src[p] = packed[0:PAIR, :]
        for peer in peers:
            pltpu.make_async_remote_copy(
                src_ref=tile_src.at[p], dst_ref=landed.at[p, mine], send_sem=ar_send.at[p], recv_sem=ar_recv.at[p],
                device_id=peer, device_id_type=MESH,
            ).start()

    def everyone(p):
        total_rows = pl.ds(0, PAIR * len(peers))
        return pltpu.make_async_remote_copy(
            src_ref=landed.at[p, total_rows], dst_ref=landed.at[p, total_rows], send_sem=ar_send.at[p],
            recv_sem=ar_recv.at[p], device_id=peers[0], device_id_type=MESH,
        )

    def mixing_of(p):
        everyone(p).wait_recv()
        parts = [landed[p, k * probes : (k + 1) * probes, :] for k in range(landed.shape[1] // probes)]
        while len(parts) > 1:
            parts = [parts[k] + parts[k + 1] if k + 1 < len(parts) else parts[k] for k in range(0, len(parts), 2)]
        packed = parts[0]
        shift = PAIR
        while shift < probes:
            packed = packed + sub_roll(packed, shift)
            shift *= 2
        grams = packed
        for q in range(1, probes // PAIR):
            grams = jnp.where(sub < PAIR * q, grams, lane_roll(packed, -q * FORMS * probes))
        diff = grams - lane_roll(grams, -probes)
        upper = jnp.where(lane < 2 * probes, diff, lane_roll(grams, 2 * probes))
        lower = jnp.where(lane < 2 * probes, lane_roll(diff, -probes), lane_roll(grams, probes))
        size = 2 * probes
        both = [upper, lower]
        scale = [jnp.sum(jnp.where(lane == sub + h * probes, both[h], 0.0), axis=1, keepdims=True) for h in range(2)]
        for k in range(size):
            h, r = k // probes, k % probes
            line = both[h][r : r + 1, :]
            pivot = line[:, k : k + 1]
            inv = jnp.where(pivot > 1e-6 * scale[h][r : r + 1, :], 1.0 / pivot, 0.0)
            line = line * inv
            for q in range(2):
                updated = both[q] - both[q][:, k : k + 1] * line
                both[q] = jnp.where(sub == r, line, updated) if q == h else updated
        pick = (lane == sub + size).astype(jnp.float32)
        return lax.dot_general(
            pick, jnp.concatenate(both, axis=0), (((1,), (1,)), ((), ())),
            precision=HIGHEST, preferred_element_type=jnp.float32,
        )

    def mix(mixing, stacked):
        return lax.dot_general(
            mixing, stacked, (((1,), (0,)), ((), ())), precision=HIGHEST, preferred_element_type=jnp.float32
        )

    prepare(0)
    for r in range(-2, rows + 2):
        h, at = where_row(r)
        main = probes_ref[:, at, :] if h == 0 else hrow[2 * per_tile : 2 * per_tile + probes, at, :]
        side = probe_strip[:, h * rows + at, :]
        for c in range(2):
            d_main, d_side = main_strip(drv, (c,), r)
            bx[0, c, r + 2, 0] = main * d_main
            bx[0, c, r + 2, 1] = side * d_side

    span = rows + 3

    def place(c, r, s):
        return pl.ds(((c * span + r + 1) * 2 + s) * lanes, lanes)

    for c in range(2):
        for r in range(-1, rows + 2):
            g = main_strip(green, (0, c, last), r)
            w = main_strip(wmx, (), r)
            m, s = b_of(0, c, r), b_of(0, c, r, 1)
            basis[0:probes, place(c, r, 0)] = (g[0] * w[0]) * m
            basis[0:probes, place(c, r, 1)] = (g[1] * w[1]) * s
            if r > rows:
                continue
            sides = [
                (b_of(0, c, r - 1), b_of(0, c, r - 1, 1)), (b_of(0, c, r + 1), b_of(0, c, r + 1, 1)),
                (south_of(m, s), south_of(s, m)), (north_of(m, s), north_of(s, m)),
            ]
            hs = [main_strip(hsc, (0, c, d, last), r) for d in DIRS]
            for k in range(2):
                x = (hs[0][k] * sides[0][k] + hs[1][k] * sides[1][k]) + (hs[2][k] * sides[2][k] + hs[3][k] * sides[3][k])
                if r == 1:
                    edge_src[c, k] = x
                basis[probes:, place(c, r, k)] = w[k] * x
    pl.when(edge_copy[2])(edge_copy[0].start)
    start_sum(0, grams_of(0))
    prepare(1)
    pl.when(edge_copy[3])(edge_copy[0].wait_recv)
    for c in range(2):
        w = main_strip(wmx, (), rows + 1)
        for k in range(2):
            basis[probes:, place(c, rows + 1, k)] = w[k] * edge_dst[c, k]
    mixing = mixing_of(0)
    mixed = mix(mixing, basis[...])
    for c in range(2):
        for r in range(-1, rows + 2):
            for k in range(2):
                start = ((c * span + r + 1) * 2 + k) * lanes
                bx[1, c, r + 2, k] = mixed[:, start : start + lanes]
    start_sum(1, grams_of(1))
    for i in range(rows):
        total = [None, None]
        for c in range(2):
            drive = drv[c, 0, pl.ds(i, 1), :]
            m, s = b_of(1, c, i), b_of(1, c, i, 1)
            around = [b_of(1, c, i - 1), b_of(1, c, i + 1), south_of(m, s), north_of(m, s)]
            terms = [hsc[1, c, d, 0, 0, pl.ds(i, 1), :] * around[d] for d in DIRS]
            parts = [
                (drive * green[1, c, 0, 0, pl.ds(i, 1), :]) * m,
                drive * ((terms[0] + terms[1]) + (terms[2] + terms[3])),
            ]
            total = [b if a is None else a + b for a, b in zip(total, parts)]
        for k in range(2):
            results[k * probes : (k + 1) * probes, pl.ds(i * lanes, lanes)] = total[k]
    mixed = mix(mixing_of(1), results[...])
    for i in range(rows):
        out_ref[:, i, :] = mixed[:, i * lanes : (i + 1) * lanes]
    for copy, _, has_dst, _ in exchange + [edge_copy]:
        pl.when(has_dst)(copy.wait_send)
    for p in range(2):
        everyone(p).wait_send()


def body(sizes, velocity, thickness, log_friction, obs_weight, ice_mask, grounded, probes):
    layers, rows, lanes = velocity.shape[1:]
    count = probes.shape[0]
    n_gx, n_gy = sizes
    fields = 2 * (layers + 1) + count + 2 + 3
    forms = 1 + 4 + 10 + 24

    def vmem(*shape):
        return pltpu.VMEM(shape, jnp.float32)

    sem = pltpu.SemaphoreType.DMA
    scratch = [
        vmem(fields, rows, lanes), vmem(fields, rows, lanes), vmem(3, 2 * rows, lanes), vmem(3, 2 * rows, lanes),
        vmem(2, 2, count, lanes), vmem(2, 2, count, lanes),
        vmem(4, layers, 4, rows, lanes), vmem(layers - 1, 4, rows, lanes), vmem(2, layers - 1, 4, rows, lanes),
        vmem(2, layers, 4, rows, lanes), vmem(2, 2, layers, 4, rows, lanes), vmem(2, 4, layers, rows, lanes),
        vmem(2, 2, 4, layers, 4, rows, lanes), vmem(2, 2, 4, layers, rows, lanes), vmem(2, 2, forms, rows, lanes),
        vmem(2, 4, rows, lanes), vmem(4, rows, lanes), vmem(count, 2 * rows, lanes),
        vmem(2, 2, rows + 4, 2, count, lanes), vmem(5, count, 2 * rows * lanes), vmem(5, 2 * count, 2 * rows * lanes),
        vmem(2 * count, 4 * (rows + 3) * lanes), vmem(2 * count, rows * lanes),
        vmem(2, PAIR, lanes), vmem(2, PAIR * n_gx * n_gy, lanes),
        sem((9,)), sem((9,)), sem((2,)), sem((2,)),
    ]
    return pl.pallas_call(
        functools.partial(kernel, sizes),
        out_shape=jax.ShapeDtypeStruct(probes.shape, jnp.float32),
        in_specs=[pl.BlockSpec(memory_space=pltpu.VMEM)] * 7,
        out_specs=pl.BlockSpec(memory_space=pltpu.VMEM),
        scratch_shapes=scratch,
        compiler_params=pltpu.CompilerParams(collective_id=0, has_side_effects=True),
        name="hessian_probe",
    )(velocity, thickness, log_friction, obs_weight, ice_mask, grounded, probes)


def solution(mesh):
    sizes = (mesh.shape["gx"], mesh.shape["gy"])
    in_specs = (
        P(None, None, "gx", "gy"),
        P("gx", "gy"),
        P("gx", "gy"),
        P("gx", "gy"),
        P("gx", "gy"),
        P("gx", "gy"),
        P(None, "gx", "gy"),
    )
    out_specs = P(None, "gx", "gy")
    return jax.shard_map(
        functools.partial(body, sizes), mesh=mesh, in_specs=in_specs, out_specs=out_specs, check_vma=False
    )
```

time: 43.8 us -> 31.2 us (0.71)
  Pallas kernels: 42.2 us -> 29.6 us
    pallas_call x1, Pallas kernels: 42.2 us -> 29.6 us  [body(): pl.pallas_call(functools.partial(kernel, sizes), out_shape=jax.ShapeDtype...]
where the time goes in v1:
time: 31.2 us; the launch traced here: 31 us
  Pallas kernels  29.6 us (95%)
  local copies, waits for them, and re-layouts  1.38 us (4%)
    pallas_call x1, Pallas kernels, body(): pl.pallas_call(functools.partial(kernel, sizes), out_shape=jax.ShapeDtype...  29.6 us
    unnamed x1, local copies, waits for them, and re-layouts  1.38 us

profile of v1, /device:TPU:0, one launch (start us, length us, event | category | flops | bytes accessed | tf_op | source)
XLA Modules:
  0.0 31.0 jit_solution(11958110276991392105)
XLA Ops:
  0.0 29.6 %hessian_probe.1 = f32[8,8,128]{2,1,0:T(8,128)} custom-call(f32[2,11,8,128]{3,2,1,0:T(8,128)} %vel_ref.1, f32[8,128]{1,0:T(8,128)} %thick_ref.1, f32[8,128]{1,0:T(8,128)} %logf_ref.1, f32[8,128]{1,0:T(8,128)} %obs_ref.1, s32[8,128]{1,0:T(8,128)} %ice_ref.1, s32[8,128]{1,0:T(8,128)} %ground_ref.1, f32[8,8,128]{2,1,0:T(8,128)} %probes_ref.1), custom_call_target="tpu_custom_call" | custom-call | tf_op jit(solution)/shard_map/hessian_probe/pallas_call | solution.py:582
  29.6 1.4 %copy.9 = f32[8,8,128]{2,1,0:T(8,128)} copy(f32[8,8,128]{2,1,0:T(8,128)} %hessian_probe.1) | data formatting | bytes 65536

commit v2 on v1

--- a/solution.py
+++ b/solution.py
@@ -21,6 +21,13 @@
 FORMS = 4
 
 
+def rounds_of(count):
+    rounds = 0
+    while 2 ** (rounds + 1) < count - 1:
+        rounds += 1
+    return rounds
+
+
 class Field:
     def __init__(self, tiles):
         self.tiles = tiles
@@ -48,14 +55,24 @@
 
 def kernel(
     sizes,
+    vel_hbm, thick_hbm, logf_hbm, obs_hbm, ice_hbm, ground_hbm, probes_hbm,
+    out_ref,
     vel_ref, thick_ref, logf_ref, obs_ref, ice_ref, ground_ref, probes_ref,
-    out_ref,
     row, hrow, tn, ts, edge_src, edge_dst,
     coef, kzs, ratio, inverse, green, wsc, hsc, hshift, quad, drv, wmx, probe_strip,
     bx, left, right, basis, results, tile_src, landed,
-    send_sem, recv_sem, ar_send, ar_recv,
+    send_sem, recv_sem, ar_send, ar_recv, in_sem, greet_sem,
 ):
     n_gx, n_gy = sizes
+    loads = [
+        pltpu.make_async_copy(src, dst, in_sem.at[k])
+        for k, (src, dst) in enumerate((
+            (vel_hbm, vel_ref), (probes_hbm, probes_ref), (thick_hbm, thick_ref), (logf_hbm, logf_ref),
+            (obs_hbm, obs_ref), (ice_hbm, ice_ref), (ground_hbm, ground_ref),
+        ))
+    ]
+    for copy in loads:
+        copy.start()
     layers = vel_ref.shape[1]
     rows = vel_ref.shape[2]
     lanes = vel_ref.shape[3]
@@ -80,9 +97,6 @@
     peers = [
         {"gx": lax.rem(ix + step // n_gy, n_gx), "gy": lax.rem(iy + step % n_gy, n_gy)} for step in range(1, n_gx * n_gy)
     ]
-    for peer in peers:
-        pl.semaphore_signal(barrier, inc=1, device_id=peer, device_id_type=MESH)
-
     def lane_roll(t, shift):
         shift = shift % lanes
         return t if shift == 0 else pltpu.roll(t, shift, 1)
@@ -93,9 +107,9 @@
     def inside(dx, dy):
         tests = []
         if dx:
-            tests.append(ix > 0 if dx < 0 else ix < n_gx - 1)
+            tests.append(ix >= -dx if dx < 0 else ix < n_gx - dx)
         if dy:
-            tests.append(iy > 0 if dy < 0 else iy < n_gy - 1)
+            tests.append(iy >= -dy if dy < 0 else iy < n_gy - dy)
         return functools.reduce(jnp.logical_and, tests)
 
     def transfer(k, dx, dy, src, dst):
@@ -110,6 +124,17 @@
         )
         return copy, dst, inside(dx, dy), inside(-dx, -dy)
 
+    for dy in (0, -1, 1, -2, 2):
+        for step in range(n_gx):
+            if step == 0 and dy == 0:
+                continue
+            target = {"gx": lax.rem(ix + step, n_gx), "gy": iy + dy}
+            if dy == 0:
+                pl.semaphore_signal(barrier, inc=1, device_id=target, device_id_type=MESH)
+            else:
+                @pl.when(inside(0, dy))
+                def _(target=target):
+                    pl.semaphore_signal(barrier, inc=1, device_id=target, device_id_type=MESH)
     low, top = pl.ds(0, half), pl.ds(half, half)
     corner_low, corner_top = pl.ds(rows, half), pl.ds(rows + half, half)
     own_pack = pl.ds(n_fields, 3)
@@ -128,6 +153,8 @@
     ]
     edge_copy = transfer(8, -1, 0, edge_src, edge_dst)
 
+    for copy in loads:
+        copy.wait()
     mask_own = ice_ref[...].astype(jnp.float32)
     friction_own = mask_own * ground_ref[...].astype(jnp.float32) * jnp.exp(logf_ref[...])
     wm_own = obs_ref[...] * mask_own
@@ -147,9 +174,30 @@
         @pl.when(jnp.logical_not(has_src))
         def _(dst=dst):
             dst[...] = jnp.zeros(dst.shape, jnp.float32)
-    pl.semaphore_wait(barrier, len(peers))
+    within = sum(inside(0, dy).astype(jnp.int32) for dy in (-1, 1, -2, 2)) + 1
+    pl.semaphore_wait(barrier, n_gx * within - 1)
     for copy, _, has_dst, _ in exchange:
         pl.when(has_dst)(copy.start)
+
+    def greet(k):
+        for dy in (-(2 ** (k + 1)), 2 ** (k + 1)):
+            @pl.when(inside(0, dy))
+            def _(dy=dy):
+                pl.semaphore_signal(greet_sem.at[k], inc=1, device_id={"gy": iy + dy}, device_id_type=MESH)
+
+    def meet(k):
+        if k < rounds:
+            reach = 2 ** (k + 1)
+            pl.semaphore_wait(
+                greet_sem.at[k], inside(0, -reach).astype(jnp.int32) + inside(0, reach).astype(jnp.int32)
+            )
+        if k + 1 < rounds:
+            greet(k + 1)
+
+    rounds = rounds_of(n_gy)
+    if rounds:
+        greet(0)
+    meet(0)
     for copy, _, _, has_src in exchange:
         pl.when(has_src)(copy.wait_recv)
 
@@ -256,6 +304,9 @@
     def load(ref, index, count=4):
         return Field([ref[index + (k,)] if k < count else None for k in range(4)])
 
+    def scale_of(c, d):
+        return ANISO_X[c] if d in (WEST, EAST) else ANISO_Y[c]
+
     for c in range(2):
         store(drv, (c,), friction * velocity[c * layers])
     store(wmx, (), wm)
@@ -272,15 +323,16 @@
         k_e = (mu + neighbour(mu, EAST)) * mask_e
         k_n = (mu + neighbour(mu, NORTH)) * mask_n
         for d, f in ((WEST, neighbour(k_e, WEST)), (EAST, k_e), (SOUTH, neighbour(k_n, SOUTH)), (NORTH, k_n)):
-            store(coef, (d, l), f)
+            for c in range(2):
+                store(coef, (c, d, l), f if scale_of(c, d) == 1.0 else scale_of(c, d) * f)
         if l < last:
             store(kzs, (l,), (mu + visc[l + 1]) * step2)
 
     for c in range(2):
         ratios, inverses = [], []
         for l in range(layers):
-            k = [load(coef, (d, l)) for d in DIRS]
-            pivot = ANISO_X[c] * (k[WEST] + k[EAST]) + ANISO_Y[c] * (k[SOUTH] + k[NORTH]) + diag
+            k = [load(coef, (c, d, l)) for d in DIRS]
+            pivot = (k[WEST] + k[EAST]) + (k[SOUTH] + k[NORTH]) + diag
             if l == 0:
                 pivot = pivot + friction
             if l > 0:
@@ -310,11 +362,10 @@
     def prepare(p):
         src = 0 if p == 0 else last
         for c in range(2):
-            scale = (ANISO_X[c], ANISO_X[c], ANISO_Y[c], ANISO_Y[c])
             for d in DIRS:
                 y = []
                 for l in range(layers):
-                    w = scale[d] * (load(coef, (d, l)) * neighbour(load(green, (p, c, l)), d))
+                    w = load(coef, (c, d, l)) * neighbour(load(green, (p, c, l)), d)
                     wsc[c, d, l] = w.tiles[0]
                     if p == 1:
                         w = Field(w.tiles[:3] + [None])
@@ -325,7 +376,7 @@
                 for l in range(last, -1, -1):
                     if l < last:
                         x = Field((y[l] + load(ratio, (c, l)) * x).tiles[:3] + [None])
-                    store(hsc, (p, c, d, l), x)
+                    store(hsc, (p, c, d, l), x if p == 0 and l == last else Field(x.tiles[:1] + [None] * 3))
                     hshift[c, 0, d, l] = sub_roll(jnp.where(sub_first, x.tiles[1], x.tiles[0]), -1)
                     hshift[c, 1, d, l] = lane_roll(jnp.where(lane_first, x.tiles[2], x.tiles[0]), -1)
             quad[p, c, 0] = green[p, c, src, 0]
@@ -344,8 +395,8 @@
                 total = [None] * 6
                 for l in range(layers):
                     h = hsc[p, c, d, l, 0]
-                    t_e = (ANISO_X[c] * coef[EAST, l, 0]) * h
-                    t_n = (ANISO_Y[c] * coef[NORTH, l, 0]) * h
+                    t_e = coef[c, EAST, l, 0] * h
+                    t_n = coef[c, NORTH, l, 0] * h
                     he = [hshift[c, 0, e, l] for e in DIRS]
                     hn = [hshift[c, 1, e, l] for e in DIRS]
                     terms = [
@@ -373,10 +424,23 @@
     def b_of(p, c, r, s=0):
         return bx[p, c, r + 2, s]
 
+    def remainder(t):
+        return t - t.astype(jnp.bfloat16).astype(jnp.float32)
+
+    def halves(t):
+        return jnp.concatenate([t, remainder(t)], axis=0).astype(jnp.bfloat16)
+
+    def at_k(block, c, i):
+        return pl.ds(((block * 2 + c) * rows + i) * lanes, lanes)
+
+    def put(block, c, i, one, two):
+        t = jnp.concatenate([one, two], axis=0)
+        right[0 : 2 * probes, at_k(block, c, i)] = t.astype(jnp.bfloat16)
+        right[2 * probes :, at_k(block, c, i)] = remainder(t).astype(jnp.bfloat16)
+
     def grams_of(p):
         for c in range(2):
             for i in range(rows):
-                k = pl.ds((c * rows + i) * lanes, lanes)
                 q = quad.at[p, c]
 
                 def row_of(index):
@@ -388,10 +452,9 @@
                 n_2 = lane_roll(jnp.where(lane < 2, b_of(p, c, i, 1), b0), -2)
                 around = [b_of(p, c, i - 1), b_of(p, c, i + 1), s_0, n_0]
                 far = [b0, b_of(p, c, i + 2), s_e, n_e, n_w, n_2]
-                left[0, :, k] = b0
-                right[0, 0:probes, k] = row_of(0) * b0
+                left[:, at_k(0, c, i)] = halves(b0)
                 first = [row_of(1 + d) * around[d] for d in DIRS]
-                right[0, probes:, k] = (first[0] + first[1]) + (first[2] + first[3])
+                put(0, c, i, row_of(0) * b0, (first[0] + first[1]) + (first[2] + first[3]))
                 at = 1 + len(DIRS)
                 cross = {}
                 for d in DIRS:
@@ -399,21 +462,24 @@
                         cross[d, e] = cross[e, d] = row_of(at)
                         at += 1
                 for d in DIRS:
-                    left[1 + d, :, k] = around[d]
+                    left[:, at_k(1 + d, c, i)] = halves(around[d])
                     terms = [cross[d, e] * around[e] for e in DIRS]
-                    right[1 + d, 0:probes, k] = (terms[0] + terms[1]) + (terms[2] + terms[3])
+                    near = (terms[0] + terms[1]) + (terms[2] + terms[3])
                     terms = [row_of(at + j) * far[j] for j in range(6)]
                     at += 6
-                    right[1 + d, probes:, k] = (terms[0] + terms[1]) + (terms[2] + terms[3]) + (terms[4] + terms[5])
-        dots = [
-            lax.dot_general(
-                left[k], right[k], (((1,), (1,)), ((), ())), precision=HIGHEST, preferred_element_type=jnp.float32
+                    put(1 + d, c, i, near, (terms[0] + terms[1]) + (terms[2] + terms[3]) + (terms[4] + terms[5]))
+        cut = 2 * rows * lanes
+
+        def contract(at, size):
+            both = lax.dot_general(
+                left[:, pl.ds(at, size)], right[:, pl.ds(at, size)], (((1,), (1,)), ((), ())),
+                preferred_element_type=jnp.float32,
             )
-            for k in range(5)
-        ]
-        outer = (dots[1] + dots[2]) + (dots[3] + dots[4])
+            both = both[0:probes, :] + both[probes:, :]
+            return both[:, 0 : 2 * probes] + both[:, 2 * probes :]
+
         pad = jnp.zeros((probes, lanes - FORMS * probes), jnp.float32)
-        return jnp.concatenate([dots[0], outer, pad], axis=1)
+        return jnp.concatenate([contract(0, cut), contract(cut, 4 * cut), pad], axis=1)
 
     def start_sum(p, grams):
         base = (FORMS - 1) * probes
@@ -498,14 +564,20 @@
     def place(c, r, s):
         return pl.ds(((c * span + r + 1) * 2 + s) * lanes, lanes)
 
+    def fill(c, r, s, one, two):
+        t = jnp.concatenate([one, two], axis=0)
+        basis[0 : 2 * probes, place(c, r, s)] = t.astype(jnp.bfloat16)
+        basis[2 * probes :, place(c, r, s)] = remainder(t).astype(jnp.bfloat16)
+
+    edge_plain = [None, None]
     for c in range(2):
         for r in range(-1, rows + 2):
             g = main_strip(green, (0, c, last), r)
             w = main_strip(wmx, (), r)
             m, s = b_of(0, c, r), b_of(0, c, r, 1)
-            basis[0:probes, place(c, r, 0)] = (g[0] * w[0]) * m
-            basis[0:probes, place(c, r, 1)] = (g[1] * w[1]) * s
+            plain = [(g[0] * w[0]) * m, (g[1] * w[1]) * s]
             if r > rows:
+                edge_plain[c] = plain
                 continue
             sides = [
                 (b_of(0, c, r - 1), b_of(0, c, r - 1, 1)), (b_of(0, c, r + 1), b_of(0, c, r + 1, 1)),
@@ -516,17 +588,25 @@
                 x = (hs[0][k] * sides[0][k] + hs[1][k] * sides[1][k]) + (hs[2][k] * sides[2][k] + hs[3][k] * sides[3][k])
                 if r == 1:
                     edge_src[c, k] = x
-                basis[probes:, place(c, r, k)] = w[k] * x
+                fill(c, r, k, plain[k], w[k] * x)
     pl.when(edge_copy[2])(edge_copy[0].start)
-    start_sum(0, grams_of(0))
+    grams = grams_of(0)
+    for k in range(1, rounds):
+        meet(k)
+    start_sum(0, grams)
     prepare(1)
     pl.when(edge_copy[3])(edge_copy[0].wait_recv)
     for c in range(2):
         w = main_strip(wmx, (), rows + 1)
         for k in range(2):
-            basis[probes:, place(c, rows + 1, k)] = w[k] * edge_dst[c, k]
+            fill(c, rows + 1, k, edge_plain[c][k], w[k] * edge_dst[c, k])
     mixing = mixing_of(0)
-    mixed = mix(mixing, basis[...])
+    mixing = jnp.concatenate([mixing, mixing], axis=1)
+    mixed = lax.dot_general(
+        jnp.concatenate([mixing, remainder(mixing)], axis=0).astype(jnp.bfloat16), basis[...],
+        (((1,), (0,)), ((), ())), preferred_element_type=jnp.float32,
+    )
+    mixed = mixed[0:probes, :] + mixed[probes:, :]
     for c in range(2):
         for r in range(-1, rows + 2):
             for k in range(2):
@@ -568,21 +648,26 @@
 
     sem = pltpu.SemaphoreType.DMA
     scratch = [
+        vmem(*velocity.shape), vmem(rows, lanes), vmem(rows, lanes), vmem(rows, lanes),
+        pltpu.VMEM((rows, lanes), jnp.int32), pltpu.VMEM((rows, lanes), jnp.int32), vmem(*probes.shape),
         vmem(fields, rows, lanes), vmem(fields, rows, lanes), vmem(3, 2 * rows, lanes), vmem(3, 2 * rows, lanes),
         vmem(2, 2, count, lanes), vmem(2, 2, count, lanes),
-        vmem(4, layers, 4, rows, lanes), vmem(layers - 1, 4, rows, lanes), vmem(2, layers - 1, 4, rows, lanes),
+        vmem(2, 4, layers, 4, rows, lanes), vmem(layers - 1, 4, rows, lanes), vmem(2, layers - 1, 4, rows, lanes),
         vmem(2, layers, 4, rows, lanes), vmem(2, 2, layers, 4, rows, lanes), vmem(2, 4, layers, rows, lanes),
         vmem(2, 2, 4, layers, 4, rows, lanes), vmem(2, 2, 4, layers, rows, lanes), vmem(2, 2, forms, rows, lanes),
         vmem(2, 4, rows, lanes), vmem(4, rows, lanes), vmem(count, 2 * rows, lanes),
-        vmem(2, 2, rows + 4, 2, count, lanes), vmem(5, count, 2 * rows * lanes), vmem(5, 2 * count, 2 * rows * lanes),
-        vmem(2 * count, 4 * (rows + 3) * lanes), vmem(2 * count, rows * lanes),
+        vmem(2, 2, rows + 4, 2, count, lanes),
+        pltpu.VMEM((2 * count, 10 * rows * lanes), jnp.bfloat16), pltpu.VMEM((4 * count, 10 * rows * lanes), jnp.bfloat16),
+
+        pltpu.VMEM((4 * count, 4 * (rows + 3) * lanes), jnp.bfloat16), vmem(2 * count, rows * lanes),
         vmem(2, PAIR, lanes), vmem(2, PAIR * n_gx * n_gy, lanes),
-        sem((9,)), sem((9,)), sem((2,)), sem((2,)),
+        sem((9,)), sem((9,)), sem((2,)), sem((2,)), sem((7,)),
+        pltpu.SemaphoreType.REGULAR((max(rounds_of(n_gy), 1),)),
     ]
     return pl.pallas_call(
         functools.partial(kernel, sizes),
-        out_shape=jax.ShapeDtypeStruct(probes.shape, jnp.float32),
-        in_specs=[pl.BlockSpec(memory_space=pltpu.VMEM)] * 7,
+        out_shape=pltpu.VMEM(probes.shape, jnp.float32),
+        in_specs=[pl.BlockSpec(memory_space=pltpu.HBM)] * 7,
         out_specs=pl.BlockSpec(memory_space=pltpu.VMEM),
         scratch_shapes=scratch,
         compiler_params=pltpu.CompilerParams(collective_id=0, has_side_effects=True),

time: 31.2 us -> 25.6 us (0.82)
  Pallas kernels: 29.6 us -> 24.8 us
  local copies, waits for them, and re-layouts: 1.38 us -> 0.62 us
    pallas_call x1, Pallas kernels: 29.6 us -> 24.8 us  [body(): pl.pallas_call(functools.partial(kernel, sizes), out_shape=pltpu.VMEM(pro...]
    unnamed x1, local copies, waits for them, and re-layouts: 1.38 us -> 0.62 us
where the time goes in v2:
time: 25.6 us; the launch traced here: 25.4 us
  Pallas kernels  24.8 us (97%)
  local copies, waits for them, and re-layouts  0.62 us (2%)
    pallas_call x1, Pallas kernels, body(): pl.pallas_call(functools.partial(kernel, sizes), out_shape=pltpu.VMEM(pro...  24.8 us
    unnamed x1, local copies, waits for them, and re-layouts  0.62 us

profile of v2, /device:TPU:0, one launch (start us, length us, event | category | flops | bytes accessed | tf_op | source)
XLA Modules:
  0.0 25.4 jit_solution(2824635147508169373)
XLA Ops:
  0.0 24.8 %hessian_probe.1 = f32[8,8,128]{2,1,0:T(8,128)S(1)} custom-call(f32[2,11,8,128]{3,2,1,0:T(8,128)} %vel_hbm.1, f32[8,128]{1,0:T(8,128)} %thick_hbm.1, f32[8,128]{1,0:T(8,128)} %logf_hbm.1, f32[8,128]{1,0:T(8,128)} %obs_hbm.1, s32[8,128]{1,0:T(8,128)} %ice_hbm.1, s32[8,128]{1,0:T(8,128)} %ground_hbm.1, f32[8,8,128]{2,1,0:T(8,128)} %probes_hbm.1), custom_call_target="tpu_custom_call" | custom-call | tf_op jit(solution)/shard_map/hessian_probe/pallas_call | solution.py:667
  24.8 0.6 %copy.9 = f32[8,8,128]{2,1,0:T(8,128)} copy(f32[8,8,128]{2,1,0:T(8,128)S(1)} %hessian_probe.1) | data formatting | bytes 65536

commit v3 on v2

--- a/solution.py
+++ b/solution.py
@@ -59,11 +59,12 @@
     out_ref,
     vel_ref, thick_ref, logf_ref, obs_ref, ice_ref, ground_ref, probes_ref,
     row, hrow, tn, ts, edge_src, edge_dst,
-    coef, kzs, ratio, inverse, green, wsc, hsc, hshift, quad, drv, wmx, probe_strip,
-    bx, left, right, basis, results, tile_src, landed,
+    coef, kzs, ratio, inverse, green, kept_ref, quad, drv, wmx, probe_strip,
+    bx, left_0, right_0, left_1, right_1, results, mixed, tile_0, tile_1, landed_0, landed_1,
     send_sem, recv_sem, ar_send, ar_recv, in_sem, greet_sem,
 ):
     n_gx, n_gy = sizes
+    lefts, rights, tile_src, landed = (left_0, left_1), (right_0, right_1), (tile_0, tile_1), (landed_0, landed_1)
     loads = [
         pltpu.make_async_copy(src, dst, in_sem.at[k])
         for k, (src, dst) in enumerate((
@@ -151,7 +152,11 @@
         transfer(6, -1, 1, row.at[own_pack, low], ts.at[packs, corner_low]),
         transfer(7, 1, 1, row.at[own_pack, top], ts.at[packs, corner_top]),
     ]
-    edge_copy = transfer(8, -1, 0, edge_src, edge_dst)
+    ahead, behind = pl.ds(0, 2), pl.ds(2, 1)
+    edges = [
+        transfer(8, -1, 0, edge_src.at[ahead], edge_dst.at[ahead]),
+        transfer(9, 1, 0, edge_src.at[behind], edge_dst.at[behind]),
+    ]
 
     for copy in loads:
         copy.wait()
@@ -170,7 +175,7 @@
             packed = moved if packed is None else jnp.where(slot_id == s, moved, packed)
         row[n_fields + k] = packed
 
-    for _, dst, _, has_src in exchange + [edge_copy]:
+    for _, dst, _, has_src in exchange + edges:
         @pl.when(jnp.logical_not(has_src))
         def _(dst=dst):
             dst[...] = jnp.zeros(dst.shape, jnp.float32)
@@ -360,52 +365,53 @@
             store(green, (1, c, l), from_top)
 
     def prepare(p):
-        src = 0 if p == 0 else last
+        src, kept = (0, last) if p == 0 else (last, 0)
         for c in range(2):
-            for d in DIRS:
-                y = []
-                for l in range(layers):
-                    w = load(coef, (c, d, l)) * neighbour(load(green, (p, c, l)), d)
-                    wsc[c, d, l] = w.tiles[0]
-                    if p == 1:
-                        w = Field(w.tiles[:3] + [None])
-                    if l > 0:
-                        w = w + load(kzs, (l - 1,)) * y[-1]
-                    y.append(w * load(inverse, (c, l)))
-                x = y[last]
-                for l in range(last, -1, -1):
-                    if l < last:
-                        x = Field((y[l] + load(ratio, (c, l)) * x).tiles[:3] + [None])
-                    store(hsc, (p, c, d, l), x if p == 0 and l == last else Field(x.tiles[:1] + [None] * 3))
-                    hshift[c, 0, d, l] = sub_roll(jnp.where(sub_first, x.tiles[1], x.tiles[0]), -1)
-                    hshift[c, 1, d, l] = lane_roll(jnp.where(lane_first, x.tiles[2], x.tiles[0]), -1)
             quad[p, c, 0] = green[p, c, src, 0]
-            for d in DIRS:
-                quad[p, c, 1 + d] = hsc[p, c, d, src, 0]
+            cross = {}
+            ys = []
+            for l in range(layers):
+                g = load(green, (p, c, l))
+                inv = load(inverse, (c, l), 3)
+                f = [load(coef, (c, d, l), 3) * neighbour(g, d) for d in DIRS]
+                if l > 0:
+                    below = load(kzs, (l - 1,), 3)
+                    f = [f[d] + below * ys[-1][d] for d in DIRS]
+                ys.append([f[d] * inv for d in DIRS])
+                for d in DIRS:
+                    for e in range(d, 4):
+                        term = f[d].tiles[0] * ys[-1][e].tiles[0]
+                        cross[d, e] = cross[d, e] + term if l > 0 else term
             at = 1 + len(DIRS)
-            for d in DIRS:
-                for e in range(d, 4):
-                    total = None
-                    for l in range(layers):
-                        term = wsc[c, d, l] * hsc[p, c, e, l, 0]
-                        total = term if total is None else total + term
-                    quad[p, c, at] = total
-                    at += 1
-            for d in DIRS:
-                total = [None] * 6
-                for l in range(layers):
-                    h = hsc[p, c, d, l, 0]
-                    t_e = coef[c, EAST, l, 0] * h
-                    t_n = coef[c, NORTH, l, 0] * h
-                    he = [hshift[c, 0, e, l] for e in DIRS]
-                    hn = [hshift[c, 1, e, l] for e in DIRS]
+            for term in cross.values():
+                quad[p, c, at] = term
+                at += 1
+            x = ys[last]
+            total = [[None] * 6 for _ in DIRS]
+            for l in range(last, -1, -1):
+                if l < last:
+                    r = load(ratio, (c, l), 3)
+                    x = [ys[l][d] + r * x[d] for d in DIRS]
+                if l == kept:
+                    for d in DIRS:
+                        for k in (0, 2):
+                            kept_ref[p, c, d, k] = x[d].tiles[k]
+                if l == src:
+                    for d in DIRS:
+                        quad[p, c, 1 + d] = x[d].tiles[0]
+                he = [sub_roll(jnp.where(sub_first, x[e].tiles[1], x[e].tiles[0]), -1) for e in DIRS]
+                hn = [lane_roll(jnp.where(lane_first, x[e].tiles[2], x[e].tiles[0]), -1) for e in DIRS]
+                k_e, k_n = coef[c, EAST, l, 0], coef[c, NORTH, l, 0]
+                for d in DIRS:
+                    t_e, t_n = k_e * x[d].tiles[0], k_n * x[d].tiles[0]
                     terms = [
                         t_e * he[WEST] + t_n * hn[SOUTH], t_e * he[EAST], t_e * he[SOUTH],
                         t_e * he[NORTH] + t_n * hn[EAST], t_n * hn[WEST], t_n * hn[NORTH],
                     ]
-                    total = [b if a is None else a + b for a, b in zip(total, terms)]
+                    total[d] = [v if u is None else u + v for u, v in zip(total[d], terms)]
+            for d in DIRS:
                 for k in range(6):
-                    quad[p, c, at] = total[k]
+                    quad[p, c, at] = total[d][k]
                     at += 1
 
     def where_row(r):
@@ -433,55 +439,135 @@
     def at_k(block, c, i):
         return pl.ds(((block * 2 + c) * rows + i) * lanes, lanes)
 
-    def put(block, c, i, one, two):
-        t = jnp.concatenate([one, two], axis=0)
-        right[0 : 2 * probes, at_k(block, c, i)] = t.astype(jnp.bfloat16)
-        right[2 * probes :, at_k(block, c, i)] = remainder(t).astype(jnp.bfloat16)
-
-    def grams_of(p):
-        for c in range(2):
-            for i in range(rows):
-                q = quad.at[p, c]
-
-                def row_of(index):
-                    return q[index, pl.ds(i, 1), :]
-
-                b0 = b_of(p, c, i)
-                n_w, n_0, n_e = (north_of(b_of(p, c, i + d), b_of(p, c, i + d, 1)) for d in (-1, 0, 1))
-                s_0, s_e = (south_of(b_of(p, c, i + d), b_of(p, c, i + d, 1)) for d in (0, 1))
-                n_2 = lane_roll(jnp.where(lane < 2, b_of(p, c, i, 1), b0), -2)
-                around = [b_of(p, c, i - 1), b_of(p, c, i + 1), s_0, n_0]
-                far = [b0, b_of(p, c, i + 2), s_e, n_e, n_w, n_2]
-                left[:, at_k(0, c, i)] = halves(b0)
-                first = [row_of(1 + d) * around[d] for d in DIRS]
-                put(0, c, i, row_of(0) * b0, (first[0] + first[1]) + (first[2] + first[3]))
-                at = 1 + len(DIRS)
-                cross = {}
-                for d in DIRS:
-                    for e in range(d, 4):
-                        cross[d, e] = cross[e, d] = row_of(at)
-                        at += 1
-                for d in DIRS:
-                    left[:, at_k(1 + d, c, i)] = halves(around[d])
-                    terms = [cross[d, e] * around[e] for e in DIRS]
-                    near = (terms[0] + terms[1]) + (terms[2] + terms[3])
-                    terms = [row_of(at + j) * far[j] for j in range(6)]
-                    at += 6
-                    put(1 + d, c, i, near, (terms[0] + terms[1]) + (terms[2] + terms[3]) + (terms[4] + terms[5]))
+    def bases_of(p):
+        return (0,) if p == 0 else (1, 2)
+
+    def put_left(p, block, c, i, parts):
+        if p == 0:
+            lefts[p][:, at_k(block, c, i)] = halves(parts[0])
+        else:
+            t = jnp.concatenate(parts, axis=0)
+            lefts[p][0 : 2 * probes, at_k(block, c, i)] = t.astype(jnp.bfloat16)
+            lefts[p][2 * probes :, at_k(block, c, i)] = remainder(t).astype(jnp.bfloat16)
+
+    def put_right(p, block, c, i, one, two):
+        step = 2 * probes
+        both = one + two
+        groups = [jnp.concatenate(both[n : n + 2], axis=0) for n in range(0, len(both), 2)]
+        for n, t in enumerate(groups):
+            rights[p][n * step : (n + 1) * step, at_k(block, c, i)] = t.astype(jnp.bfloat16)
+            m = n + len(groups)
+            rights[p][m * step : (m + 1) * step, at_k(block, c, i)] = remainder(t).astype(jnp.bfloat16)
+
+    def tree(terms):
+        while len(terms) > 1:
+            terms = [terms[n] + terms[n + 1] if n + 1 < len(terms) else terms[n] for n in range(0, len(terms), 2)]
+        return terms[0]
+
+    def stencil_row(p, c, i):
+        q = quad.at[p, c]
+
+        def row_of(index):
+            return q[index, pl.ds(i, 1), :]
+
+        count = 1 + len(DIRS)
+        cross = {}
+        for d in DIRS:
+            for e in range(d, 4):
+                cross[d, e] = cross[e, d] = row_of(count)
+                count += 1
+        ones, twos, arounds, centres = [[] for _ in range(5)], [[] for _ in range(5)], [], []
+        for n in bases_of(p):
+            b0 = b_of(n, c, i)
+            n_w, n_0, n_e = (north_of(b_of(n, c, i + d), b_of(n, c, i + d, 1)) for d in (-1, 0, 1))
+            s_0, s_e = (south_of(b_of(n, c, i + d), b_of(n, c, i + d, 1)) for d in (0, 1))
+            n_2 = lane_roll(jnp.where(lane < 2, b_of(n, c, i, 1), b0), -2)
+            around = [b_of(n, c, i - 1), b_of(n, c, i + 1), s_0, n_0]
+            far = [b0, b_of(n, c, i + 2), s_e, n_e, n_w, n_2]
+            centres.append(b0)
+            arounds.append(around)
+            ones[0].append(row_of(0) * b0)
+            twos[0].append(tree([row_of(1 + d) * around[d] for d in DIRS]))
+            for d in DIRS:
+                ones[1 + d].append(tree([cross[d, e] * around[e] for e in DIRS]))
+                twos[1 + d].append(tree([row_of(count + 6 * d + j) * far[j] for j in range(6)]))
+        put_left(p, 0, c, i, centres)
+        for d in DIRS:
+            put_left(p, 1 + d, c, i, [around[d] for around in arounds])
+        for block in range(5):
+            put_right(p, block, c, i, ones[block], twos[block])
+
+    def contract(p):
         cut = 2 * rows * lanes
-
-        def contract(at, size):
+        size = probes * len(bases_of(p))
+        results = []
+        for at, span in ((0, cut), (cut, 4 * cut)):
             both = lax.dot_general(
-                left[:, pl.ds(at, size)], right[:, pl.ds(at, size)], (((1,), (1,)), ((), ())),
+                lefts[p][:, pl.ds(at, span)], rights[p][:, pl.ds(at, span)], (((1,), (1,)), ((), ())),
                 preferred_element_type=jnp.float32,
             )
-            both = both[0:probes, :] + both[probes:, :]
-            return both[:, 0 : 2 * probes] + both[:, 2 * probes :]
-
-        pad = jnp.zeros((probes, lanes - FORMS * probes), jnp.float32)
-        return jnp.concatenate([contract(0, cut), contract(cut, 4 * cut), pad], axis=1)
-
-    def start_sum(p, grams):
+            both = both[0:size, :] + both[size:, :]
+            results.append(both[:, 0 : 2 * size] + both[:, 2 * size :])
+        return jnp.concatenate(results, axis=1)
+
+    width = FORMS * probes
+
+    def start_sum(p, tile_rows, packed):
+        mine = pl.ds((ix * n_gy + iy) * tile_rows, tile_rows)
+        landed[p][mine, :] = packed
+        tile_src[p][...] = packed
+        for peer in peers:
+            pltpu.make_async_remote_copy(
+                src_ref=tile_src[p], dst_ref=landed[p].at[mine], send_sem=ar_send.at[p], recv_sem=ar_recv.at[p],
+                device_id=peer, device_id_type=MESH,
+            ).start()
+
+    def everyone(p):
+        total_rows = pl.ds(0, (PAIR, rows)[p] * len(peers))
+        return pltpu.make_async_remote_copy(
+            src_ref=landed[p].at[total_rows], dst_ref=landed[p].at[total_rows], send_sem=ar_send.at[p],
+            recv_sem=ar_recv.at[p], device_id=peers[0], device_id_type=MESH,
+        )
+
+    def start_first():
+        grams = jnp.concatenate([contract(0), jnp.zeros((probes, lanes - width), jnp.float32)], axis=1)
+        packed = grams
+        for q in range(1, probes // PAIR):
+            packed = jnp.where(lane < q * width, packed, lane_roll(sub_roll(grams, -PAIR * q), q * width))
+        start_sum(0, PAIR, packed[0:PAIR, :])
+
+    def start_second():
+        forms = contract(1)
+        start_sum(1, rows, jnp.concatenate([forms[0:probes, :], forms[probes:, :]], axis=1))
+
+    def landed_sum(p):
+        return tree([landed[p][k * probes : (k + 1) * probes, :] for k in range(landed[p].shape[0] // probes)])
+
+    def first_grams():
+        packed = landed_sum(0)
+        shift = PAIR
+        while shift < probes:
+            packed = packed + sub_roll(packed, shift)
+            shift *= 2
+        grams = packed
+        for q in range(1, probes // PAIR):
+            grams = jnp.where(sub < PAIR * q, grams, lane_roll(packed, -q * width))
+        return grams
+
+    def dot(a, b, dims):
+        return lax.dot_general(a, b, (dims, ((), ())), precision=HIGHEST, preferred_element_type=jnp.float32)
+
+    def second_grams(mixing):
+        forms = landed_sum(1)
+        size = 2 * probes
+        forms = jnp.concatenate([forms[:, 0 : FORMS * size], forms[:, FORMS * size :]], axis=0)
+        half_mixed = dot(mixing, forms, ((1,), (0,)))
+        stacked = jnp.concatenate([half_mixed[:, f * size : (f + 1) * size] for f in range(FORMS)], axis=0)
+        full = dot(stacked, mixing, ((1,), (1,)))
+        parts = [full[f * probes : (f + 1) * probes, :] for f in range(FORMS)]
+        return jnp.concatenate(parts + [jnp.zeros((probes, lanes - width), jnp.float32)], axis=1)
+
+    def mixing_of(grams):
         base = (FORMS - 1) * probes
         mirrored = grams
         for r in range(probes):
@@ -490,39 +576,6 @@
             )
             mirrored = jnp.where(lane == base + r, grams + column, mirrored)
         grams = mirrored
-        width = FORMS * probes
-        packed = grams
-        for q in range(1, probes // PAIR):
-            packed = jnp.where(lane < q * width, packed, lane_roll(sub_roll(grams, -PAIR * q), q * width))
-        mine = pl.ds((ix * n_gy + iy) * PAIR, PAIR)
-        landed[p, mine, :] = packed[0:PAIR, :]
-        tile_src[p] = packed[0:PAIR, :]
-        for peer in peers:
-            pltpu.make_async_remote_copy(
-                src_ref=tile_src.at[p], dst_ref=landed.at[p, mine], send_sem=ar_send.at[p], recv_sem=ar_recv.at[p],
-                device_id=peer, device_id_type=MESH,
-            ).start()
-
-    def everyone(p):
-        total_rows = pl.ds(0, PAIR * len(peers))
-        return pltpu.make_async_remote_copy(
-            src_ref=landed.at[p, total_rows], dst_ref=landed.at[p, total_rows], send_sem=ar_send.at[p],
-            recv_sem=ar_recv.at[p], device_id=peers[0], device_id_type=MESH,
-        )
-
-    def mixing_of(p):
-        everyone(p).wait_recv()
-        parts = [landed[p, k * probes : (k + 1) * probes, :] for k in range(landed.shape[1] // probes)]
-        while len(parts) > 1:
-            parts = [parts[k] + parts[k + 1] if k + 1 < len(parts) else parts[k] for k in range(0, len(parts), 2)]
-        packed = parts[0]
-        shift = PAIR
-        while shift < probes:
-            packed = packed + sub_roll(packed, shift)
-            shift *= 2
-        grams = packed
-        for q in range(1, probes // PAIR):
-            grams = jnp.where(sub < PAIR * q, grams, lane_roll(packed, -q * FORMS * probes))
         diff = grams - lane_roll(grams, -probes)
         upper = jnp.where(lane < 2 * probes, diff, lane_roll(grams, 2 * probes))
         lower = jnp.where(lane < 2 * probes, lane_roll(diff, -probes), lane_roll(grams, probes))
@@ -539,15 +592,7 @@
                 updated = both[q] - both[q][:, k : k + 1] * line
                 both[q] = jnp.where(sub == r, line, updated) if q == h else updated
         pick = (lane == sub + size).astype(jnp.float32)
-        return lax.dot_general(
-            pick, jnp.concatenate(both, axis=0), (((1,), (1,)), ((), ())),
-            precision=HIGHEST, preferred_element_type=jnp.float32,
-        )
-
-    def mix(mixing, stacked):
-        return lax.dot_general(
-            mixing, stacked, (((1,), (0,)), ((), ())), precision=HIGHEST, preferred_element_type=jnp.float32
-        )
+        return dot(pick, jnp.concatenate(both, axis=0), ((1,), (1,)))
 
     prepare(0)
     for r in range(-2, rows + 2):
@@ -559,78 +604,80 @@
             bx[0, c, r + 2, 0] = main * d_main
             bx[0, c, r + 2, 1] = side * d_side
 
-    span = rows + 3
-
-    def place(c, r, s):
-        return pl.ds(((c * span + r + 1) * 2 + s) * lanes, lanes)
-
-    def fill(c, r, s, one, two):
-        t = jnp.concatenate([one, two], axis=0)
-        basis[0 : 2 * probes, place(c, r, s)] = t.astype(jnp.bfloat16)
-        basis[2 * probes :, place(c, r, s)] = remainder(t).astype(jnp.bfloat16)
-
-    edge_plain = [None, None]
+    def surface(c, r):
+        m, s = b_of(0, c, r), b_of(0, c, r, 1)
+        sides = [
+            (b_of(0, c, r - 1), b_of(0, c, r - 1, 1)), (b_of(0, c, r + 1), b_of(0, c, r + 1, 1)),
+            (south_of(m, s), south_of(s, m)), (north_of(m, s), north_of(s, m)),
+        ]
+        hs = [main_strip(kept_ref, (0, c, d), r) for d in DIRS]
+        return [tree([hs[d][k] * sides[d][k] for d in DIRS]) for k in range(2)]
+
+    sent_rows = (0, 1, rows - 1)
+    got_rows = (rows, rows + 1, -1)
+    for n, r in enumerate(sent_rows):
+        for c in range(2):
+            x = surface(c, r)
+            for k in range(2):
+                edge_src[n, c, k] = x[k]
+    for copy, _, has_dst, _ in edges:
+        pl.when(has_dst)(copy.start)
     for c in range(2):
-        for r in range(-1, rows + 2):
-            g = main_strip(green, (0, c, last), r)
-            w = main_strip(wmx, (), r)
-            m, s = b_of(0, c, r), b_of(0, c, r, 1)
-            plain = [(g[0] * w[0]) * m, (g[1] * w[1]) * s]
-            if r > rows:
-                edge_plain[c] = plain
-                continue
-            sides = [
-                (b_of(0, c, r - 1), b_of(0, c, r - 1, 1)), (b_of(0, c, r + 1), b_of(0, c, r + 1, 1)),
-                (south_of(m, s), south_of(s, m)), (north_of(m, s), north_of(s, m)),
-            ]
-            hs = [main_strip(hsc, (0, c, d, last), r) for d in DIRS]
-            for k in range(2):
-                x = (hs[0][k] * sides[0][k] + hs[1][k] * sides[1][k]) + (hs[2][k] * sides[2][k] + hs[3][k] * sides[3][k])
-                if r == 1:
-                    edge_src[c, k] = x
-                fill(c, r, k, plain[k], w[k] * x)
-    pl.when(edge_copy[2])(edge_copy[0].start)
-    grams = grams_of(0)
+        for i in range(rows):
+            stencil_row(0, c, i)
     for k in range(1, rounds):
         meet(k)
-    start_sum(0, grams)
+    start_first()
     prepare(1)
-    pl.when(edge_copy[3])(edge_copy[0].wait_recv)
+
+    def fill_row(c, r, x):
+        g = main_strip(green, (0, c, last), r)
+        w = main_strip(wmx, (), r)
+        for k in range(2):
+            bx[1, c, r + 2, k] = (g[k] * w[k]) * b_of(0, c, r, k)
+            bx[2, c, r + 2, k] = w[k] * x[k]
+
+    inner = range(1, rows - 2)
     for c in range(2):
-        w = main_strip(wmx, (), rows + 1)
-        for k in range(2):
-            fill(c, rows + 1, k, edge_plain[c][k], w[k] * edge_dst[c, k])
-    mixing = mixing_of(0)
-    mixing = jnp.concatenate([mixing, mixing], axis=1)
-    mixed = lax.dot_general(
-        jnp.concatenate([mixing, remainder(mixing)], axis=0).astype(jnp.bfloat16), basis[...],
-        (((1,), (0,)), ((), ())), preferred_element_type=jnp.float32,
-    )
-    mixed = mixed[0:probes, :] + mixed[probes:, :]
+        for r in range(rows):
+            fill_row(c, r, [edge_src[sent_rows.index(r), c, k] for k in range(2)] if r in sent_rows else surface(c, r))
     for c in range(2):
-        for r in range(-1, rows + 2):
+        for i in inner:
+            stencil_row(1, c, i)
+    for copy, _, _, has_src in edges:
+        pl.when(has_src)(copy.wait_recv)
+    for n, r in enumerate(got_rows):
+        for c in range(2):
+            fill_row(c, r, [edge_dst[n, c, k] for k in range(2)])
+    for c in range(2):
+        for i in range(rows):
+            if i not in inner:
+                stencil_row(1, c, i)
+    start_second()
+    for i in range(rows):
+        at = pl.ds(i * lanes, lanes)
+        for n in bases_of(1):
+            total = [None, None]
+            for c in range(2):
+                drive = drv[c, 0, pl.ds(i, 1), :]
+                m, s = b_of(n, c, i), b_of(n, c, i, 1)
+                around = [b_of(n, c, i - 1), b_of(n, c, i + 1), south_of(m, s), north_of(m, s)]
+                parts = [
+                    (drive * green[1, c, 0, 0, pl.ds(i, 1), :]) * m,
+                    drive * tree([kept_ref[1, c, d, 0, pl.ds(i, 1), :] * around[d] for d in DIRS]),
+                ]
+                total = [b if a is None else a + b for a, b in zip(total, parts)]
             for k in range(2):
-                start = ((c * span + r + 1) * 2 + k) * lanes
-                bx[1, c, r + 2, k] = mixed[:, start : start + lanes]
-    start_sum(1, grams_of(1))
+                results[k, (n - 1) * probes : n * probes, at] = total[k]
+    everyone(0).wait_recv()
+    mixing = mixing_of(first_grams())
+    for k in range(2):
+        mixed[k * probes : (k + 1) * probes, :] = dot(mixing, results[k], ((1,), (0,)))
+    everyone(1).wait_recv()
+    final = dot(mixing_of(second_grams(mixing)), mixed[...], ((1,), (0,)))
     for i in range(rows):
-        total = [None, None]
-        for c in range(2):
-            drive = drv[c, 0, pl.ds(i, 1), :]
-            m, s = b_of(1, c, i), b_of(1, c, i, 1)
-            around = [b_of(1, c, i - 1), b_of(1, c, i + 1), south_of(m, s), north_of(m, s)]
-            terms = [hsc[1, c, d, 0, 0, pl.ds(i, 1), :] * around[d] for d in DIRS]
-            parts = [
-                (drive * green[1, c, 0, 0, pl.ds(i, 1), :]) * m,
-                drive * ((terms[0] + terms[1]) + (terms[2] + terms[3])),
-            ]
-            total = [b if a is None else a + b for a, b in zip(total, parts)]
-        for k in range(2):
-            results[k * probes : (k + 1) * probes, pl.ds(i * lanes, lanes)] = total[k]
-    mixed = mix(mixing_of(1), results[...])
-    for i in range(rows):
-        out_ref[:, i, :] = mixed[:, i * lanes : (i + 1) * lanes]
-    for copy, _, has_dst, _ in exchange + [edge_copy]:
+        out_ref[:, i, :] = final[:, i * lanes : (i + 1) * lanes]
+    for copy, _, has_dst, _ in exchange + edges:
         pl.when(has_dst)(copy.wait_send)
     for p in range(2):
         everyone(p).wait_send()
@@ -646,22 +693,25 @@
     def vmem(*shape):
         return pltpu.VMEM(shape, jnp.float32)
 
+    def half(*shape):
+        return pltpu.VMEM(shape, jnp.bfloat16)
+
     sem = pltpu.SemaphoreType.DMA
     scratch = [
         vmem(*velocity.shape), vmem(rows, lanes), vmem(rows, lanes), vmem(rows, lanes),
         pltpu.VMEM((rows, lanes), jnp.int32), pltpu.VMEM((rows, lanes), jnp.int32), vmem(*probes.shape),
         vmem(fields, rows, lanes), vmem(fields, rows, lanes), vmem(3, 2 * rows, lanes), vmem(3, 2 * rows, lanes),
-        vmem(2, 2, count, lanes), vmem(2, 2, count, lanes),
+        vmem(3, 2, 2, count, lanes), vmem(3, 2, 2, count, lanes),
         vmem(2, 4, layers, 4, rows, lanes), vmem(layers - 1, 4, rows, lanes), vmem(2, layers - 1, 4, rows, lanes),
-        vmem(2, layers, 4, rows, lanes), vmem(2, 2, layers, 4, rows, lanes), vmem(2, 4, layers, rows, lanes),
-        vmem(2, 2, 4, layers, 4, rows, lanes), vmem(2, 2, 4, layers, rows, lanes), vmem(2, 2, forms, rows, lanes),
+        vmem(2, layers, 4, rows, lanes), vmem(2, 2, layers, 4, rows, lanes),
+        vmem(2, 2, 4, 4, rows, lanes), vmem(2, 2, forms, rows, lanes),
         vmem(2, 4, rows, lanes), vmem(4, rows, lanes), vmem(count, 2 * rows, lanes),
-        vmem(2, 2, rows + 4, 2, count, lanes),
-        pltpu.VMEM((2 * count, 10 * rows * lanes), jnp.bfloat16), pltpu.VMEM((4 * count, 10 * rows * lanes), jnp.bfloat16),
-
-        pltpu.VMEM((4 * count, 4 * (rows + 3) * lanes), jnp.bfloat16), vmem(2 * count, rows * lanes),
-        vmem(2, PAIR, lanes), vmem(2, PAIR * n_gx * n_gy, lanes),
-        sem((9,)), sem((9,)), sem((2,)), sem((2,)), sem((7,)),
+        vmem(3, 2, rows + 4, 2, count, lanes),
+        half(2 * count, 10 * rows * lanes), half(4 * count, 10 * rows * lanes),
+        half(4 * count, 10 * rows * lanes), half(8 * count, 10 * rows * lanes),
+        vmem(2, 2 * count, rows * lanes), vmem(2 * count, rows * lanes),
+        vmem(PAIR, lanes), vmem(rows, lanes), vmem(PAIR * n_gx * n_gy, lanes), vmem(rows * n_gx * n_gy, lanes),
+        sem((10,)), sem((10,)), sem((2,)), sem((2,)), sem((7,)),
         pltpu.SemaphoreType.REGULAR((max(rounds_of(n_gy), 1),)),
     ]
     return pl.pallas_call(

time: 25.6 us -> 23.3 us (0.910)
  Pallas kernels: 24.8 us -> 22.5 us
    pallas_call x1, Pallas kernels: 24.8 us -> 22.5 us  [body(): pl.pallas_call(functools.partial(kernel, sizes), out_shape=pltpu.VMEM(pro...]
where the time goes in v3:
time: 23.3 us; the launch traced here: 23.2 us
  Pallas kernels  22.5 us (97%)
  local copies, waits for them, and re-layouts  0.62 us (3%)
    pallas_call x1, Pallas kernels, body(): pl.pallas_call(functools.partial(kernel, sizes), out_shape=pltpu.VMEM(pro...  22.5 us
    unnamed x1, local copies, waits for them, and re-layouts  0.62 us

profile of v3, /device:TPU:0, one launch (start us, length us, event | category | flops | bytes accessed | tf_op | source)
XLA Modules:
  0.0 23.2 jit_solution(11177965904425459295)
XLA Ops:
  0.0 22.5 %hessian_probe.1 = f32[8,8,128]{2,1,0:T(8,128)S(1)} custom-call(f32[2,11,8,128]{3,2,1,0:T(8,128)} %vel_hbm.1, f32[8,128]{1,0:T(8,128)} %thick_hbm.1, f32[8,128]{1,0:T(8,128)} %logf_hbm.1, f32[8,128]{1,0:T(8,128)} %obs_hbm.1, s32[8,128]{1,0:T(8,128)} %ice_hbm.1, s32[8,128]{1,0:T(8,128)} %ground_hbm.1, f32[8,8,128]{2,1,0:T(8,128)} %probes_hbm.1), custom_call_target="tpu_custom_call" | custom-call | tf_op jit(solution)/shard_map/hessian_probe/pallas_call | solution.py:717
  22.5 0.6 %copy.9 = f32[8,8,128]{2,1,0:T(8,128)} copy(f32[8,8,128]{2,1,0:T(8,128)S(1)} %hessian_probe.1) | data formatting | bytes 65536

commit v4 on v3

--- a/solution.py
+++ b/solution.py
@@ -175,14 +175,14 @@
             packed = moved if packed is None else jnp.where(slot_id == s, moved, packed)
         row[n_fields + k] = packed
 
+    within = sum(inside(0, dy).astype(jnp.int32) for dy in (-1, 1, -2, 2)) + 1
+    pl.semaphore_wait(barrier, n_gx * within - 1)
+    for copy, _, has_dst, _ in exchange:
+        pl.when(has_dst)(copy.start)
     for _, dst, _, has_src in exchange + edges:
         @pl.when(jnp.logical_not(has_src))
         def _(dst=dst):
             dst[...] = jnp.zeros(dst.shape, jnp.float32)
-    within = sum(inside(0, dy).astype(jnp.int32) for dy in (-1, 1, -2, 2)) + 1
-    pl.semaphore_wait(barrier, n_gx * within - 1)
-    for copy, _, has_dst, _ in exchange:
-        pl.when(has_dst)(copy.start)
 
     def greet(k):
         for dy in (-(2 ** (k + 1)), 2 ** (k + 1)):
@@ -364,10 +364,10 @@
             store(green, (0, c, l), from_bottom)
             store(green, (1, c, l), from_top)
 
-    def prepare(p):
+    def prepare(p, between=lambda: None):
         src, kept = (0, last) if p == 0 else (last, 0)
         for c in range(2):
-            quad[p, c, 0] = green[p, c, src, 0]
+            quad[p, c, 0] = 0.5 * green[p, c, src, 0]
             cross = {}
             ys = []
             for l in range(layers):
@@ -378,13 +378,14 @@
                     below = load(kzs, (l - 1,), 3)
                     f = [f[d] + below * ys[-1][d] for d in DIRS]
                 ys.append([f[d] * inv for d in DIRS])
+                between()
                 for d in DIRS:
                     for e in range(d, 4):
                         term = f[d].tiles[0] * ys[-1][e].tiles[0]
                         cross[d, e] = cross[d, e] + term if l > 0 else term
-            at = 1 + len(DIRS)
-            for term in cross.values():
-                quad[p, c, at] = term
+            at = 3
+            for (d, e), term in cross.items():
+                quad[p, c, at] = 0.5 * term if d == e else term
                 at += 1
             x = ys[last]
             total = [[None] * 6 for _ in DIRS]
@@ -392,13 +393,14 @@
                 if l < last:
                     r = load(ratio, (c, l), 3)
                     x = [ys[l][d] + r * x[d] for d in DIRS]
+                between()
                 if l == kept:
                     for d in DIRS:
                         for k in (0, 2):
                             kept_ref[p, c, d, k] = x[d].tiles[k]
                 if l == src:
-                    for d in DIRS:
-                        quad[p, c, 1 + d] = x[d].tiles[0]
+                    quad[p, c, 1] = x[EAST].tiles[0]
+                    quad[p, c, 2] = x[NORTH].tiles[0]
                 he = [sub_roll(jnp.where(sub_first, x[e].tiles[1], x[e].tiles[0]), -1) for e in DIRS]
                 hn = [lane_roll(jnp.where(lane_first, x[e].tiles[2], x[e].tiles[0]), -1) for e in DIRS]
                 k_e, k_n = coef[c, EAST, l, 0], coef[c, NORTH, l, 0]
@@ -430,34 +432,47 @@
     def b_of(p, c, r, s=0):
         return bx[p, c, r + 2, s]
 
-    def remainder(t):
-        return t - t.astype(jnp.bfloat16).astype(jnp.float32)
+    def split(t):
+        head = t.astype(jnp.bfloat16)
+        return head, (t - head.astype(jnp.float32)).astype(jnp.bfloat16)
 
     def halves(t):
-        return jnp.concatenate([t, remainder(t)], axis=0).astype(jnp.bfloat16)
+        return jnp.concatenate([t, t - t.astype(jnp.bfloat16).astype(jnp.float32)], axis=0).astype(jnp.bfloat16)
+
+    inner = list(range(1, rows - 2))
+    outer = [i for i in range(rows) if i not in inner]
+    cut = 10 * len(inner)
 
     def at_k(block, c, i):
-        return pl.ds(((block * 2 + c) * rows + i) * lanes, lanes)
+        group = inner if i in inner else outer
+        base = 0 if i in inner else cut
+        return pl.ds((base + (block * 2 + c) * len(group) + group.index(i)) * lanes, lanes)
 
     def bases_of(p):
         return (0,) if p == 0 else (1, 2)
 
-    def put_left(p, block, c, i, parts):
+    def put_left(p, places, c, parts):
+        t = jnp.concatenate(parts, axis=0)
         if p == 0:
-            lefts[p][:, at_k(block, c, i)] = halves(parts[0])
+            rounded = [halves(t)]
         else:
-            t = jnp.concatenate(parts, axis=0)
-            lefts[p][0 : 2 * probes, at_k(block, c, i)] = t.astype(jnp.bfloat16)
-            lefts[p][2 * probes :, at_k(block, c, i)] = remainder(t).astype(jnp.bfloat16)
+            rounded = split(t)
+        step = 2 * probes
+        for block, i in places:
+            if 0 <= i < rows:
+                for n, part in enumerate(rounded):
+                    lefts[p][n * step : (n + 1) * step, at_k(block, c, i)] = part
+
+    def left_row(p, c, r):
+        put_left(p, ((0, r), (1 + WEST, r + 1), (1 + EAST, r - 1)), c, [b_of(n, c, r) for n in bases_of(p)])
 
     def put_right(p, block, c, i, one, two):
         step = 2 * probes
         both = one + two
         groups = [jnp.concatenate(both[n : n + 2], axis=0) for n in range(0, len(both), 2)]
         for n, t in enumerate(groups):
-            rights[p][n * step : (n + 1) * step, at_k(block, c, i)] = t.astype(jnp.bfloat16)
-            m = n + len(groups)
-            rights[p][m * step : (m + 1) * step, at_k(block, c, i)] = remainder(t).astype(jnp.bfloat16)
+            for m, part in zip((n, n + len(groups)), split(t)):
+                rights[p][m * step : (m + 1) * step, at_k(block, c, i)] = part
 
     def tree(terms):
         while len(terms) > 1:
@@ -470,13 +485,13 @@
         def row_of(index):
             return q[index, pl.ds(i, 1), :]
 
-        count = 1 + len(DIRS)
+        count = 3
         cross = {}
         for d in DIRS:
             for e in range(d, 4):
-                cross[d, e] = cross[e, d] = row_of(count)
+                cross[d, e] = row_of(count)
                 count += 1
-        ones, twos, arounds, centres = [[] for _ in range(5)], [[] for _ in range(5)], [], []
+        ones, twos, arounds = [[] for _ in range(5)], [[] for _ in range(5)], []
         for n in bases_of(p):
             b0 = b_of(n, c, i)
             n_w, n_0, n_e = (north_of(b_of(n, c, i + d), b_of(n, c, i + d, 1)) for d in (-1, 0, 1))
@@ -484,24 +499,23 @@
             n_2 = lane_roll(jnp.where(lane < 2, b_of(n, c, i, 1), b0), -2)
             around = [b_of(n, c, i - 1), b_of(n, c, i + 1), s_0, n_0]
             far = [b0, b_of(n, c, i + 2), s_e, n_e, n_w, n_2]
-            centres.append(b0)
             arounds.append(around)
             ones[0].append(row_of(0) * b0)
-            twos[0].append(tree([row_of(1 + d) * around[d] for d in DIRS]))
+            twos[0].append(row_of(1) * around[EAST] + row_of(2) * around[NORTH])
             for d in DIRS:
-                ones[1 + d].append(tree([cross[d, e] * around[e] for e in DIRS]))
+                ones[1 + d].append(tree([cross[d, e] * around[e] for e in range(d, 4)]))
                 twos[1 + d].append(tree([row_of(count + 6 * d + j) * far[j] for j in range(6)]))
-        put_left(p, 0, c, i, centres)
-        for d in DIRS:
-            put_left(p, 1 + d, c, i, [around[d] for around in arounds])
+        for d in (SOUTH, NORTH):
+            put_left(p, ((1 + d, i),), c, [around[d] for around in arounds])
         for block in range(5):
             put_right(p, block, c, i, ones[block], twos[block])
 
-    def contract(p):
-        cut = 2 * rows * lanes
+    def contract(p, group):
         size = probes * len(bases_of(p))
         results = []
-        for at, span in ((0, cut), (cut, 4 * cut)):
+        base = (0 if group is inner else cut) * lanes
+        step = 2 * len(group) * lanes
+        for at, span in ((base, step), (base + step, 4 * step)):
             both = lax.dot_general(
                 lefts[p][:, pl.ds(at, span)], rights[p][:, pl.ds(at, span)], (((1,), (1,)), ((), ())),
                 preferred_element_type=jnp.float32,
@@ -516,11 +530,13 @@
         mine = pl.ds((ix * n_gy + iy) * tile_rows, tile_rows)
         landed[p][mine, :] = packed
         tile_src[p][...] = packed
-        for peer in peers:
+        return [
             pltpu.make_async_remote_copy(
                 src_ref=tile_src[p], dst_ref=landed[p].at[mine], send_sem=ar_send.at[p], recv_sem=ar_recv.at[p],
                 device_id=peer, device_id_type=MESH,
-            ).start()
+            )
+            for peer in peers
+        ]
 
     def everyone(p):
         total_rows = pl.ds(0, (PAIR, rows)[p] * len(peers))
@@ -529,16 +545,16 @@
             recv_sem=ar_recv.at[p], device_id=peers[0], device_id_type=MESH,
         )
 
-    def start_first():
-        grams = jnp.concatenate([contract(0), jnp.zeros((probes, lanes - width), jnp.float32)], axis=1)
+    def start_first(sums):
+        grams = widened(sums)
         packed = grams
         for q in range(1, probes // PAIR):
             packed = jnp.where(lane < q * width, packed, lane_roll(sub_roll(grams, -PAIR * q), q * width))
-        start_sum(0, PAIR, packed[0:PAIR, :])
-
-    def start_second():
-        forms = contract(1)
-        start_sum(1, rows, jnp.concatenate([forms[0:probes, :], forms[probes:, :]], axis=1))
+        return start_sum(0, PAIR, packed[0:PAIR, :])
+
+    def start_second(forms):
+        for copy in start_sum(1, rows, jnp.concatenate([forms[0:probes, :], forms[probes:, :]], axis=1)):
+            copy.start()
 
     def landed_sum(p):
         return tree([landed[p][k * probes : (k + 1) * probes, :] for k in range(landed[p].shape[0] // probes)])
@@ -552,7 +568,12 @@
         grams = packed
         for q in range(1, probes // PAIR):
             grams = jnp.where(sub < PAIR * q, grams, lane_roll(packed, -q * width))
-        return grams
+        stacked = jnp.concatenate([grams[:, f * probes : (f + 1) * probes] for f in range(FORMS)], axis=0)
+        pick = (lane == sub).astype(jnp.float32)[:, 0:probes]
+        return widened(grams[:, 0:width] + dot(pick, stacked, ((1,), (1,))))
+
+    def widened(t):
+        return jnp.concatenate([t, jnp.zeros((probes, lanes - width), jnp.float32)], axis=1)
 
     def dot(a, b, dims):
         return lax.dot_general(a, b, (dims, ((), ())), precision=HIGHEST, preferred_element_type=jnp.float32)
@@ -565,17 +586,9 @@
         stacked = jnp.concatenate([half_mixed[:, f * size : (f + 1) * size] for f in range(FORMS)], axis=0)
         full = dot(stacked, mixing, ((1,), (1,)))
         parts = [full[f * probes : (f + 1) * probes, :] for f in range(FORMS)]
-        return jnp.concatenate(parts + [jnp.zeros((probes, lanes - width), jnp.float32)], axis=1)
+        return widened(jnp.concatenate(parts, axis=1) + dot(mixing, stacked, ((1,), (1,))))
 
     def mixing_of(grams):
-        base = (FORMS - 1) * probes
-        mirrored = grams
-        for r in range(probes):
-            column = jnp.sum(
-                jnp.where(lane == base + sub, jnp.broadcast_to(grams[r : r + 1, :], tile), 0.0), axis=1, keepdims=True
-            )
-            mirrored = jnp.where(lane == base + r, grams + column, mirrored)
-        grams = mirrored
         diff = grams - lane_roll(grams, -probes)
         upper = jnp.where(lane < 2 * probes, diff, lane_roll(grams, 2 * probes))
         lower = jnp.where(lane < 2 * probes, lane_roll(diff, -probes), lane_roll(grams, probes))
@@ -591,8 +604,7 @@
             for q in range(2):
                 updated = both[q] - both[q][:, k : k + 1] * line
                 both[q] = jnp.where(sub == r, line, updated) if q == h else updated
-        pick = (lane == sub + size).astype(jnp.float32)
-        return dot(pick, jnp.concatenate(both, axis=0), ((1,), (1,)))
+        return jnp.transpose(jnp.concatenate(both, axis=0))[size : size + probes, :]
 
     prepare(0)
     for r in range(-2, rows + 2):
@@ -623,12 +635,26 @@
     for copy, _, has_dst, _ in edges:
         pl.when(has_dst)(copy.start)
     for c in range(2):
-        for i in range(rows):
+        for r in range(-1, rows + 1):
+            left_row(0, c, r)
+        for i in inner:
             stencil_row(0, c, i)
+    sums = contract(0, inner)
+    for c in range(2):
+        for i in outer:
+            stencil_row(0, c, i)
+    sums = sums + contract(0, outer)
     for k in range(1, rounds):
         meet(k)
-    start_first()
-    prepare(1)
+    waiting = start_first(sums)
+
+    def send_one():
+        if waiting:
+            waiting.pop(0).start()
+
+    prepare(1, send_one)
+    while waiting:
+        send_one()
 
     def fill_row(c, r, x):
         g = main_strip(green, (0, c, last), r)
@@ -637,23 +663,26 @@
             bx[1, c, r + 2, k] = (g[k] * w[k]) * b_of(0, c, r, k)
             bx[2, c, r + 2, k] = w[k] * x[k]
 
-    inner = range(1, rows - 2)
     for c in range(2):
         for r in range(rows):
             fill_row(c, r, [edge_src[sent_rows.index(r), c, k] for k in range(2)] if r in sent_rows else surface(c, r))
     for c in range(2):
+        for r in range(rows):
+            left_row(1, c, r)
         for i in inner:
             stencil_row(1, c, i)
     for copy, _, _, has_src in edges:
         pl.when(has_src)(copy.wait_recv)
+    sums = contract(1, inner)
     for n, r in enumerate(got_rows):
         for c in range(2):
             fill_row(c, r, [edge_dst[n, c, k] for k in range(2)])
     for c in range(2):
-        for i in range(rows):
-            if i not in inner:
-                stencil_row(1, c, i)
-    start_second()
+        left_row(1, c, -1)
+        left_row(1, c, rows)
+        for i in outer:
+            stencil_row(1, c, i)
+    start_second(sums + contract(1, outer))
     for i in range(rows):
         at = pl.ds(i * lanes, lanes)
         for n in bases_of(1):
@@ -688,7 +717,7 @@
     count = probes.shape[0]
     n_gx, n_gy = sizes
     fields = 2 * (layers + 1) + count + 2 + 3
-    forms = 1 + 4 + 10 + 24
+    forms = 1 + 2 + 10 + 24
 
     def vmem(*shape):
         return pltpu.VMEM(shape, jnp.float32)

time: 23.3 us -> 22.5 us (0.966)
  Pallas kernels: 22.5 us -> 21.7 us
    pallas_call x1, Pallas kernels: 22.5 us -> 21.7 us  [body(): pl.pallas_call(functools.partial(kernel, sizes), out_shape=pltpu.VMEM(pro...]
where the time goes in v4:
time: 22.5 us; the launch traced here: 22.3 us
  Pallas kernels  21.7 us (96%)
  local copies, waits for them, and re-layouts  0.62 us (3%)
    pallas_call x1, Pallas kernels, body(): pl.pallas_call(functools.partial(kernel, sizes), out_shape=pltpu.VMEM(pro...  21.7 us
    unnamed x1, local copies, waits for them, and re-layouts  0.62 us

profile of v4, /device:TPU:0, one launch (start us, length us, event | category | flops | bytes accessed | tf_op | source)
XLA Modules:
  0.0 22.3 jit_solution(10561658811178515136)
XLA Ops:
  0.0 21.7 %hessian_probe.1 = f32[8,8,128]{2,1,0:T(8,128)S(1)} custom-call(f32[2,11,8,128]{3,2,1,0:T(8,128)} %vel_hbm.1, f32[8,128]{1,0:T(8,128)} %thick_hbm.1, f32[8,128]{1,0:T(8,128)} %logf_hbm.1, f32[8,128]{1,0:T(8,128)} %obs_hbm.1, s32[8,128]{1,0:T(8,128)} %ice_hbm.1, s32[8,128]{1,0:T(8,128)} %ground_hbm.1, f32[8,8,128]{2,1,0:T(8,128)} %probes_hbm.1), custom_call_target="tpu_custom_call" | custom-call | tf_op jit(solution)/shard_map/hessian_probe/pallas_call | solution.py:746
  21.7 0.6 %copy.9 = f32[8,8,128]{2,1,0:T(8,128)} copy(f32[8,8,128]{2,1,0:T(8,128)S(1)} %hessian_probe.1) | data formatting | bytes 65536

commit v5 on v4

--- a/solution.py
+++ b/solution.py
@@ -96,7 +96,7 @@
 
     barrier = pltpu.get_barrier_semaphore()
     peers = [
-        {"gx": lax.rem(ix + step // n_gy, n_gx), "gy": lax.rem(iy + step % n_gy, n_gy)} for step in range(1, n_gx * n_gy)
+        {"gx": lax.rem(ix + step // n_gy, n_gx), "gy": lax.rem(iy + step % n_gy, n_gy)} for step in sorted(range(1, n_gx * n_gy), key=lambda step: -min(step % n_gy, n_gy - step % n_gy))
     ]
     def lane_roll(t, shift):
         shift = shift % lanes

time: 22.5 us -> 22.4 us (level)
  no operation moved by 1% of the time
where the time goes in v5:
time: 22.4 us; the launch traced here: 22.2 us
  Pallas kernels  21.6 us (96%)
  local copies, waits for them, and re-layouts  0.62 us (3%)
    pallas_call x1, Pallas kernels, body(): pl.pallas_call(functools.partial(kernel, sizes), out_shape=pltpu.VMEM(pro...  21.6 us
    unnamed x1, local copies, waits for them, and re-layouts  0.62 us

profile of v5, /device:TPU:0, one launch (start us, length us, event | category | flops | bytes accessed | tf_op | source)
XLA Modules:
  0.0 22.2 jit_solution(4082766752668920526)
XLA Ops:
  0.0 21.6 %hessian_probe.1 = f32[8,8,128]{2,1,0:T(8,128)S(1)} custom-call(f32[2,11,8,128]{3,2,1,0:T(8,128)} %vel_hbm.1, f32[8,128]{1,0:T(8,128)} %thick_hbm.1, f32[8,128]{1,0:T(8,128)} %logf_hbm.1, f32[8,128]{1,0:T(8,128)} %obs_hbm.1, s32[8,128]{1,0:T(8,128)} %ice_hbm.1, s32[8,128]{1,0:T(8,128)} %ground_hbm.1, f32[8,8,128]{2,1,0:T(8,128)} %probes_hbm.1), custom_call_target="tpu_custom_call" | custom-call | tf_op jit(solution)/shard_map/hessian_probe/pallas_call | solution.py:746
  21.6 0.6 %copy.9 = f32[8,8,128]{2,1,0:T(8,128)} copy(f32[8,8,128]{2,1,0:T(8,128)S(1)} %hessian_probe.1) | data formatting | bytes 65536
